TPU v7x, 128 devices: a whole 4x4x4 slice. The times are simulated.
128 devices in a mesh: req: 16 (over y, x), hid: 8 (over z, core).
Axes of the slice: x: 4, y: 4, z: 4, core: 2. Of those that a mesh axis runs over, the one named last changes fastest.
Arguments:
- tokens: bfloat16 [32, 16, 2, 4096], P('req', 'hid'), may hold values from -6 to 6
- input_gain: float32 [4096], replicated, may hold values from 0.1 to 1.9
- qkv_weight: bfloat16 [4096, 3, 4096], P(None, None, 'hid'), may hold values from -0.09375 to 0.09375
- out_weight: bfloat16 [4096, 4096], P('hid'), may hold values from -0.375 to 0.375
- in_weight: bfloat16 [4096, 16384], P(None, ('req', 'hid')), may hold values from -0.09375 to 0.09375
- down_weight: bfloat16 [16384, 4096], P(('req', 'hid')), may hold values from -0.046875 to 0.046875
- final_gain: float32 [4096], replicated, may hold values from 0.1 to 1.9
- score_weight: bfloat16 [4096], replicated, may hold values from -0.09375 to 0.09375
- prompt_keys: bfloat16 [32, 2048, 4096], P('req', None, 'hid'), may hold values from -260 to 260
- prompt_values: bfloat16 [32, 2048, 4096], P('req', None, 'hid'), may hold values from -6 to 6
- tail_keys: bfloat16 [32, 16, 64, 4096], P('req', None, None, 'hid'), may hold values from -12 to 12
- tail_values: bfloat16 [32, 16, 64, 4096], P('req', None, None, 'hid'), may hold values from -6 to 6
- prompt_lengths: int32 [32], P('req'), may hold values from 1 to 2048
- tail_lengths: int32 [32, 16], P('req'), may hold values from 0 to 64
Outputs:
- next_hidden: bfloat16 [32, 16, 2, 4096], P('req', 'hid')
- sample_scores: float32 [32, 16, 2], P('req', 'hid')
Inputs may be any that keep to these rules, and one draw needn't show every extreme that they name: `prompt_lengths`: a request's prompt occupies positions 0 to its length - 1. `tail_lengths`: a sample's tail occupies positions 0 to its length - 1.
All inputs are finite; a program needn't handle non-finite values.
Results may differ from a plain program's by a relative error of at most 0.017.
Values may be sent and summed in bfloat16 or wider, within the bound.
No kernel may reach another device: no remote copies, remote signals or barrier semaphores. Data moves between devices by JAX's collectives and lax.ppermute only.
A program may use at most 128 MiB of HBM per device.

v0:
```python
import jax
import jax.numpy as jnp
from jax import lax
from jax.sharding import PartitionSpec as P

HEAD_DIM = 256
ROT = 64


very_low = -1e30


def layer_norm(values, gain):
    centre = jnp.mean(values, axis=-1, keepdims=True)
    centred = values - centre
    spread = jnp.mean(centred * centred, axis=-1, keepdims=True)
    return centred * lax.rsqrt(spread + 1e-05) * gain


def rotate(vectors, positions):
    half_rot = ROT // 2
    frequency = 10000.0 ** (-(jnp.arange(half_rot, dtype=jnp.float32) * (2.0 / ROT)))
    angles = positions.astype(jnp.float32)[..., None] * frequency
    cosine = jnp.cos(angles)[..., None, :]
    sine_part = jnp.sin(angles)[..., None, :]
    paired = vectors[..., :ROT].reshape(vectors.shape[:-1] + (half_rot, 2))
    even_part = paired[..., 0]
    odd_part = paired[..., 1]
    turned = jnp.stack(
        [even_part * cosine - odd_part * sine_part, odd_part * cosine + even_part * sine_part],
        axis=-1,
    )
    return jnp.concatenate(
        [turned.reshape(vectors.shape[:-1] + (ROT,)), vectors[..., ROT:]], axis=-1
    )


def shards(
    tokens,
    input_gain,
    qkv_weight,
    out_weight,
    in_weight,
    down_weight,
    final_gain,
    score_weight,
    prompt_keys,
    prompt_values,
    tail_keys,
    tail_values,
    prompt_lengths,
    tail_lengths,
):
    req_dev, samp_dev, fresh, width = tokens.shape
    own_rows = req_dev * samp_dev * fresh
    residual = tokens.astype(jnp.float32).reshape(own_rows, width)
    normed = layer_norm(residual, input_gain).astype(jnp.bfloat16)
    gathered = lax.all_gather(normed, ("req", "hid"), axis=0, tiled=True)
    hidden_units = jax.nn.gelu(
        jnp.dot(gathered, in_weight, preferred_element_type=jnp.float32), approximate=True
    ).astype(jnp.bfloat16)
    slab_rows, triple, slab_cols = qkv_weight.shape
    flat_qkv = qkv_weight.reshape(slab_rows, triple * slab_cols)
    hid_count = lax.axis_size("hid")
    group_rows = own_rows * hid_count
    group_normed = lax.dynamic_slice_in_dim(
        gathered, lax.axis_index("req") * group_rows, group_rows, 0
    )
    mixed_qkv = jnp.dot(group_normed, flat_qkv, preferred_element_type=jnp.float32).astype(
        jnp.bfloat16
    )
    heads_here = slab_cols // HEAD_DIM
    samples = hid_count * samp_dev
    grouped = mixed_qkv.reshape(hid_count, req_dev, samp_dev, fresh, triple, heads_here, HEAD_DIM)
    grouped = jnp.transpose(grouped, (1, 0, 2, 3, 4, 5, 6)).reshape(
        req_dev, samples, fresh, triple, heads_here, HEAD_DIM
    )
    positions = (
        prompt_lengths[:, None, None]
        + tail_lengths[:, :, None]
        + jnp.arange(fresh, dtype=jnp.int32)[None, None, :]
    )
    queries = rotate(grouped[:, :, :, 0].astype(jnp.float32), positions).astype(jnp.bfloat16)
    new_keys = rotate(grouped[:, :, :, 1].astype(jnp.float32), positions).astype(jnp.bfloat16)
    new_values = grouped[:, :, :, 2]
    prompt_len = prompt_keys.shape[1]
    cached_keys = prompt_keys.reshape(req_dev, prompt_len, heads_here, HEAD_DIM)
    cached_values = prompt_values.reshape(req_dev, prompt_len, heads_here, HEAD_DIM)
    prompt_queries = queries.reshape(req_dev, samples * fresh, heads_here, HEAD_DIM)
    score_scale = HEAD_DIM ** (-0.5)
    prompt_scores = (
        jnp.einsum(
            "rqhd,rkhd->rqhk", prompt_queries, cached_keys, preferred_element_type=jnp.float32
        )
        * score_scale
    )
    keeping = (jnp.arange(prompt_len, dtype=jnp.int32)[None, :] < prompt_lengths[:, None])[
        :, None, None, :
    ]
    prompt_scores = jnp.where(keeping, prompt_scores, very_low)
    peaks = jnp.max(prompt_scores, axis=-1)
    prompt_weights = jnp.where(keeping, jnp.exp(prompt_scores - peaks[..., None]), 0.0)
    totals = jnp.sum(prompt_weights, axis=-1)
    accrued = jnp.einsum(
        "rqhk,rkhd->rqhd",
        prompt_weights.astype(jnp.bfloat16),
        cached_values,
        preferred_element_type=jnp.float32,
    )
    peaks = peaks.reshape(req_dev, samples, fresh, heads_here)
    totals = totals.reshape(req_dev, samples, fresh, heads_here)
    accrued = accrued.reshape(req_dev, samples, fresh, heads_here, HEAD_DIM)
    tail_len = tail_keys.shape[2]
    later_keys = tail_keys.reshape(req_dev, samples, tail_len, heads_here, HEAD_DIM)
    later_values = tail_values.reshape(req_dev, samples, tail_len, heads_here, HEAD_DIM)
    tail_scores = (
        jnp.einsum("rsthd,rskhd->rsthk", queries, later_keys, preferred_element_type=jnp.float32)
        * score_scale
    )
    tail_keep = (jnp.arange(tail_len, dtype=jnp.int32)[None, None, :] < tail_lengths[:, :, None])[
        :, :, None, None, :
    ]
    self_scores = (
        jnp.einsum("rsthd,rsuhd->rsthu", queries, new_keys, preferred_element_type=jnp.float32)
        * score_scale
    )
    position_order = jnp.arange(fresh, dtype=jnp.int32)
    self_keep = (position_order[None, :] <= position_order[:, None])[None, None, :, None, :]
    highest = jnp.maximum(peaks, jnp.max(jnp.where(tail_keep, tail_scores, very_low), axis=-1))
    highest = jnp.maximum(highest, jnp.max(jnp.where(self_keep, self_scores, very_low), axis=-1))
    scaling = jnp.exp(peaks - highest)
    tail_weights = jnp.where(tail_keep, jnp.exp(tail_scores - highest[..., None]), 0.0)
    self_weights = jnp.where(self_keep, jnp.exp(self_scores - highest[..., None]), 0.0)
    totals = totals * scaling + jnp.sum(tail_weights, axis=-1) + jnp.sum(self_weights, axis=-1)
    accrued = accrued * scaling[..., None]
    accrued = accrued + jnp.einsum(
        "rsthk,rskhd->rsthd",
        tail_weights.astype(jnp.bfloat16),
        later_values,
        preferred_element_type=jnp.float32,
    )
    accrued = accrued + jnp.einsum(
        "rsthu,rsuhd->rsthd",
        self_weights.astype(jnp.bfloat16),
        new_values,
        preferred_element_type=jnp.float32,
    )
    attended = (accrued / totals[..., None]).astype(jnp.bfloat16)
    attended = attended.reshape(req_dev, hid_count, samp_dev, fresh, heads_here * HEAD_DIM)
    attended_rows = jnp.transpose(attended, (1, 0, 2, 3, 4)).reshape(
        group_rows, heads_here * HEAD_DIM
    )
    mlp_part = lax.psum_scatter(
        jnp.dot(hidden_units, down_weight, preferred_element_type=jnp.float32),
        ("req", "hid"),
        scatter_dimension=0,
        tiled=True,
    )
    projection_part = lax.psum_scatter(
        jnp.dot(attended_rows, out_weight, preferred_element_type=jnp.float32).astype(jnp.bfloat16),
        "hid",
        scatter_dimension=0,
        tiled=True,
    ).astype(jnp.float32)
    branch_sum = mlp_part + projection_part
    final_state = residual + branch_sum
    next_hidden = final_state.astype(jnp.bfloat16).reshape(req_dev, samp_dev, fresh, width)
    sample_scores = jnp.sum(
        layer_norm(final_state, final_gain) * score_weight.astype(jnp.float32), axis=-1
    )
    return (next_hidden, sample_scores.reshape(req_dev, samp_dev, fresh))


def solution(mesh):
    placed = (
        P("req", "hid", None, None),
        P(),
        P(None, None, "hid"),
        P("hid", None),
        P(None, ("req", "hid")),
        P(("req", "hid"), None),
        P(),
        P(),
        P("req", None, "hid"),
        P("req", None, "hid"),
        P("req", None, None, "hid"),
        P("req", None, None, "hid"),
        P("req"),
        P("req", None),
    )
    return jax.shard_map(
        shards,
        mesh=mesh,
        in_specs=placed,
        out_specs=(P("req", "hid", None, None), P("req", "hid", None)),
        check_vma=False,
    )
```

profile of v0, /device:TPU:0, one launch (start us, length us, event | category | flops | bytes accessed | tf_op | source)
XLA Modules:
  0.0 822.6 jit_solution(10335013178201926168)
XLA Ops:
  7.2 0.9 reshape.217
  8.2 1.0 convert_reduce_fusion
  9.2 1.1 multiply_reduce_fusion.2
  10.2 0.1 div.23
  10.3 0.1 rsqrt.20
  10.4 1.4 multiply_convert_fusion
  11.9 0.0 reduce-scatter.5.cloned.1.call-start
  12.0 16.9 %copy.120 = bf16[4096,3,512]{0,2,1:T(8,128)(2,1)} copy(bf16[4096,3,512]{2,0,1:T(8,128)(2,1)} %param.16) | data formatting | bytes 25165824 | tf_op args[2]
  28.9 0.1 broadcast_add_fusion
  29.0 0.1 iota_compare_fusion
  29.1 0.3 multiply_cosine_fusion
  29.4 0.1 iota_compare_fusion.1
  29.5 55.2 %all-gather.2.cloned.1.call-done = bf16[1024,4096]{1,0:T(8,128)(2,1)} async-done(((bf16[8,4096]{1,0:T(8,128)(2,1)}), bf16[1024,4096]{1,0:T(8,128)(2,1)}) %all-gather.2.cloned.1.call-update) | async-done | bytes 8388624 | tf_op jit(solution)/shard_map/all_gather | solution.py:58
  84.7 8.7 %convolution_convert_fusion.1 = bf16[64,1536]{1,0:T(8,128)(2,1)S(1)} fusion(bf16[4096,1536]{0,1:T(8,128)(2,1)} %bitcast.109, bf16[1024,4096]{1,0:T(8,128)(2,1)} %all-gather.2.cloned.1.call-done, s32[]{:T(128)S(6)} %select_n.27), kind=kOutput, calls=%fused_computation.10 | convolution fusion | flops 805404672 | bytes 13303812 | tf_op jit(solution)/shard_map/dot_general | solution.py:69
  93.3 0.1 reshape.219
  93.4 0.2 copy.209
  93.6 0.1 reshape.220
  93.7 0.1 slice.72
  93.8 0.1 slice.55
  93.9 0.1 copy.122
  94.1 0.3 multiply_subtract_fusion
  94.4 0.4 maximum_convert_fusion
  94.8 2.0 copy.123
  96.8 0.1 copy.128
  96.9 0.1 copy.133
  97.0 0.3 subtract_convert_fusion
  97.4 0.4 pad_maximum_fusion
  97.7 0.1 copy.134
  97.9 0.1 copy.124
  97.9 0.1 pad_maximum_fusion.1
  98.0 0.2 fusion.65
  98.2 0.1 copy.137
  98.4 2.4 select_reduce_fusion
  100.7 0.1 copy.132
  100.8 1.9 concatenate.16
  102.8 3.6 fusion.85
  106.4 0.1 reshape.225
  106.5 0.1 copy.140
  106.6 0.1 fusion.70
  106.7 0.1 copy.143
  106.8 0.1 fusion.83
  106.9 0.3 fusion.73
  107.2 0.1 copy.148
  107.3 0.3 fusion.39
  107.6 0.1 reshape.232
  107.7 0.1 copy.147
  107.8 0.1 copy.141
  107.9 3.0 fusion.21
  111.0 0.1 reshape.224
  111.1 0.1 copy.151
  111.2 0.1 copy.146
  111.3 2.0 fusion.29
  113.4 0.2 fusion.32
  113.7 4.1 convolution_convert_fusion
  117.8 0.0 reduce-scatter.3.cloned.1.call-start
  117.8 14.4 %fusion.54 = f32[1024,4096]{1,0:T(8,128)} fusion(bf16[128,4096]{1,0:T(8,128)(2,1)S(1)} %copy-done, bf16[1024,4096]{1,0:T(8,128)(2,1)} %all-gather.2.cloned.1.call-done, bf16[4096,128]{1,0:T(8,128)(2,1)S(1)} %copy-done.1), kind=kOutput, calls=%fused_computation.42 | convolution fusion | flops 2148663296 | bytes 27262976 | tf_op jit(solution)/shard_map/dot_general | solution.py:154
  132.2 0.7 copy-done.3
  132.9 13.7 %reduce-scatter.5.cloned.1.call-done = bf16[8,4096]{1,0:T(8,128)(2,1)} async-done(((bf16[64,4096]{1,0:T(8,128)(2,1)}), bf16[8,4096]{1,0:T(8,128)(2,1)}) %reduce-scatter.5.cloned.1.call-update) | async-done | bytes 65552 | tf_op jit(solution)/shard_map/reduce_scatter | solution.py:159
  146.6 666.6 %reduce-scatter.3.cloned.1.call-done = f32[8,4096]{1,0:T(8,128)} async-done(((f32[1024,4096]{1,0:T(8,128)}), f32[8,4096]{1,0:T(8,128)}) %reduce-scatter.3.cloned.1.call-update) | async-done | bytes 131088 | tf_op jit(solution)/shard_map/reduce_scatter | solution.py:153
  813.2 1.1 fusion.84
  814.2 0.2 multiply_reduce_fusion.1
  814.5 0.2 multiply_reduce_fusion
  814.7 0.7 reshape.235
  815.4 0.7 reshape.236
  (31 shorter events, 0.3 us)
Async XLA Ops:
  7.2 110.6 %copy-start = (bf16[128,4096]{1,0:T(8,128)(2,1)S(1)}, bf16[128,4096]{1,0:T(8,128)(2,1)}, u32[]{:S(2)}) copy-start(bf16[128,4096]{1,0:T(8,128)(2,1)} %param.19) | copy-start | bytes 3145732
  7.2 77.5 %all-gather.2.cloned.1.call-start = ((), (), s32[]{:S(2)}) async-start(), calls=%async_computation.2 | async-start | bytes 8454144 | tf_op jit(solution)/shard_map/all_gather | solution.py:58
  11.9 134.7 %reduce-scatter.5.cloned.1.call-start = ((), (), s32[]{:S(2)}) async-start(), calls=%async_computation.4 | async-start | bytes 589824 | tf_op jit(solution)/shard_map/reduce_scatter | solution.py:159
  11.9 17.0 %copy-start.4 = (s32[2,16]{1,0:T(2,128)S(1)}, s32[2,16]{1,0:T(2,128)}, u32[]{:S(2)}) copy-start(s32[2,16]{1,0:T(2,128)} %param.27) | copy-start | bytes 388
  11.9 17.0 %copy-start.5 = (s32[2]{0:T(128)S(1)}, s32[2]{0:T(128)}, u32[]{:S(2)}) copy-start(s32[2]{0:T(128)} %param.26) | copy-start | bytes 28
  113.3 4.5 copy-start.1
  117.8 695.4 %reduce-scatter.3.cloned.1.call-start = ((), (), s32[]{:S(2)}) async-start(), calls=%async_computation.3 | async-start | bytes 16908288 | tf_op jit(solution)/shard_map/reduce_scatter | solution.py:153
  132.2 0.7 copy-start.3
  132.2 682.2 %copy-start.2 = (f32[4096]{0:T(1024)S(1)}, f32[4096]{0:T(1024)}, u32[]{:S(2)}) copy-start(f32[4096]{0:T(1024)} %param.20) | copy-start | bytes 49156
Sparse Core Ops, SparseCore 0:
  12.0 72.6 all-gather.1
  117.9 28.6 reduce-scatter.4
  149.1 664.0 reduce-scatter.2
where the time goes:
time: 823 us
  waiting for transfers between devices  735 us (89%)
  matrix products  38.6 us (5%)
  local copies, waits for them, and re-layouts  26.3 us (3%)
  between operations  14.1 us (2%)
    reduce_scatter x1, waiting for transfers between devices, shards(): lax.psum_scatter(jnp.dot(hidden_units, down_weight, preferred_element_typ...  667 us
    all_gather x1, waiting for transfers between devices, shards(): gathered = lax.all_gather(normed, ('req', 'hid'), axis=0, tiled=True)  55.2 us
    unnamed x13, local copies, waits for them, and re-layouts  17.6 us
  transfers between devices with their start and end apart: 3, of which 3 were waited for; matrix products, arithmetic and copies ran while one was open for 4% of the time, Pallas kernels for 0%

commit v1 on v0

v1 whole, which is shorter than its diff:
```python
import jax
import jax.numpy as jnp
from jax import lax
from jax.experimental import pallas as pl
from jax.experimental.pallas import tpu as pltpu
from jax.sharding import Mesh
from jax.sharding import PartitionSpec as P

HEAD_DIM = 256
ROT = 64
VERY_LOW = -1e30
SIDE = 4
CORES = 2
AXES = ("y", "x", "u", "w", "c")
REQ = ("y", "x")
HID = ("u", "w", "c")


def device_at(y, x, z, core):
    return (((y % SIDE) * SIDE + x % SIDE) * SIDE + z % SIDE) * CORES + core


def places():
    for y in range(SIDE):
        for x in range(SIDE):
            for z in range(SIDE):
                for core in range(CORES):
                    yield y, x, z, core


def token_groups():
    groups = {}
    for y, x, z, core in places():
        groups.setdefault(((x + z) % 2, (y + z) % 2, core), []).append(device_at(y, x, z, core))
    return [sorted(group) for group in groups.values()]


def from_neighbour(values, axis):
    moves = []
    for y, x, z, core in places():
        step = 1 - 2 * core
        target = device_at(
            y + step * (axis == "y"), x + step * (axis == "x"), z + step * (axis == "z"), core
        )
        moves.append((device_at(y, x, z, core), target))
    return lax.ppermute(values, AXES, moves)


def swap(values, axis):
    return lax.ppermute(values, axis, [(0, 1), (1, 0)])


def layer_norm(values, gain):
    centre = jnp.mean(values, axis=-1, keepdims=True)
    centred = values - centre
    spread = jnp.mean(centred * centred, axis=-1, keepdims=True)
    return centred * lax.rsqrt(spread + 1e-05) * gain


def rotation_tables(positions):
    half_rot = ROT // 2
    frequency = 10000.0 ** (-(jnp.arange(half_rot, dtype=jnp.float32) * (2.0 / ROT)))
    angles = positions.astype(jnp.float32)[..., None] * jnp.repeat(frequency, 2)
    sign = jnp.where(jnp.arange(ROT) % 2 == 0, -1.0, 1.0)
    rest = [(0, 0)] * (angles.ndim - 1) + [(0, HEAD_DIM - ROT)]
    return (
        jnp.pad(jnp.cos(angles), rest, constant_values=1.0),
        jnp.pad(jnp.sin(angles) * sign, rest),
    )


def qkv_body(rows_ref, weight_ref, out_ref):
    out_ref[0] = jnp.dot(
        rows_ref[...], weight_ref[0], preferred_element_type=jnp.float32
    ).astype(jnp.bfloat16)


def qkv_call(rows, weight):
    count, width = rows.shape
    triple, _, columns = weight.shape
    return pl.pallas_call(
        qkv_body,
        out_shape=jax.ShapeDtypeStruct((triple, count, columns), jnp.bfloat16),
        grid=(triple, columns // HEAD_DIM),
        in_specs=[
            pl.BlockSpec((count, width), lambda i, j: (0, 0)),
            pl.BlockSpec((1, width, HEAD_DIM), lambda i, j: (i, 0, j)),
        ],
        out_specs=pl.BlockSpec((1, count, HEAD_DIM), lambda i, j: (i, 0, j)),
        cost_estimate=pl.CostEstimate(
            flops=2 * count * width * triple * columns,
            bytes_accessed=2 * width * triple * columns,
            transcendentals=0,
        ),
        name="qkv",
    )(rows, weight)


def attention_body(
    meta_ref, qkv_ref, cos_ref, sin_ref, tails_ref, pk_ref, pv_ref, tk_ref, tv_ref, wo_ref, out_ref, acc_ref
):
    head, request = pl.program_id(0), pl.program_id(1)
    prompt_len = meta_ref[request]
    hid = meta_ref[2]
    count = qkv_ref.shape[1]
    here = cos_ref.shape[1]
    row = lax.broadcasted_iota(jnp.int32, (here, count), 0)
    col = lax.broadcasted_iota(jnp.int32, (here, count), 1)
    block = col >> 3
    owner = hid ^ (((block & 1) << 2) | (block & 2) | (block >> 2))
    pick = (((col >> 2) & 1) == request) & (owner == (row >> 2)) & ((col & 3) == (row & 3))
    pick = jnp.where(pick, 1.0, 0.0).astype(jnp.bfloat16)

    def chosen(part):
        return jnp.dot(pick, qkv_ref[part], preferred_element_type=jnp.float32)

    even = lax.broadcasted_iota(jnp.int32, (here, HEAD_DIM), 1) % 2 == 0

    def turned(part):
        values = chosen(part)
        other = jnp.where(
            even, pltpu.roll(values, HEAD_DIM - 1, 1), pltpu.roll(values, 1, 1)
        )
        return (values * cos_ref[0] + other * sin_ref[0]).astype(jnp.bfloat16)

    queries, new_keys = turned(0), turned(1)
    new_values = chosen(2).astype(jnp.bfloat16)
    scale = HEAD_DIM ** (-0.5)

    def scores(keys):
        return (
            lax.dot_general(
                queries, keys, (((1,), (1,)), ((), ())), preferred_element_type=jnp.float32
            )
            * scale
        )

    def places_of(shape):
        return lax.broadcasted_iota(jnp.int32, shape, 0), lax.broadcasted_iota(jnp.int32, shape, 1)

    prompt = scores(pk_ref[0])
    _, at = places_of(prompt.shape)
    prompt = jnp.where(at < prompt_len, prompt, VERY_LOW)
    tail = scores(tk_ref[0])
    line, at = places_of(tail.shape)
    tail_len = tk_ref.shape[1] // (here // 2)
    keep = (at // tail_len == line // 2) & (at % tail_len < tails_ref[0])
    tail = jnp.where(keep, tail, VERY_LOW)
    fresh = scores(new_keys)
    line, at = places_of(fresh.shape)
    fresh = jnp.where((at // 2 == line // 2) & (at <= line), fresh, VERY_LOW)
    top = jnp.maximum(
        jnp.max(prompt, axis=1, keepdims=True),
        jnp.maximum(jnp.max(tail, axis=1, keepdims=True), jnp.max(fresh, axis=1, keepdims=True)),
    )
    total = jnp.zeros((here, 1), jnp.float32)
    summed = jnp.zeros((here, HEAD_DIM), jnp.float32)
    for part, values in ((prompt, pv_ref[0]), (tail, tv_ref[0]), (fresh, new_values)):
        weights = jnp.exp(part - top)
        total = total + jnp.sum(weights, axis=1, keepdims=True)
        summed = summed + jnp.dot(
            weights.astype(jnp.bfloat16), values, preferred_element_type=jnp.float32
        )
    attended = (summed / total).astype(jnp.bfloat16)
    placed = lax.dot_general(
        pick, attended, (((0,), (0,)), ((), ())), preferred_element_type=jnp.float32
    ).astype(jnp.bfloat16)
    term = jnp.dot(placed, wo_ref[...], preferred_element_type=jnp.float32)

    @pl.when((head == 0) & (request == 0))
    def _():
        acc_ref[...] = term

    @pl.when((head > 0) | (request > 0))
    def _():
        acc_ref[...] += term

    @pl.when((head == pl.num_programs(0) - 1) & (request == pl.num_programs(1) - 1))
    def _():
        out_ref[...] = acc_ref[...].astype(jnp.bfloat16)


def attention_call(meta, qkv, cosine, sine, tails, pk, pv, tk, tv, wo):
    triple, count, columns = qkv.shape
    requests, prompt_len, _ = pk.shape
    here = cosine.shape[1]
    width = wo.shape[1]
    keys = prompt_len + tk.shape[1]
    whole = lambda h, r, m: (r, 0, 0)
    cached = lambda h, r, m: (r, 0, h)
    return pl.pallas_call(
        attention_body,
        out_shape=jax.ShapeDtypeStruct((count, width), jnp.bfloat16),
        grid_spec=pltpu.PrefetchScalarGridSpec(
            num_scalar_prefetch=1,
            grid=(columns // HEAD_DIM, requests),
            in_specs=[
                pl.BlockSpec((triple, count, HEAD_DIM), lambda h, r, m: (0, 0, h)),
                pl.BlockSpec((1, here, HEAD_DIM), whole),
                pl.BlockSpec((1, here, HEAD_DIM), whole),
                pl.BlockSpec((1, here, 1), whole),
                pl.BlockSpec((1, prompt_len, HEAD_DIM), cached),
                pl.BlockSpec((1, prompt_len, HEAD_DIM), cached),
                pl.BlockSpec((1, tk.shape[1], HEAD_DIM), cached),
                pl.BlockSpec((1, tk.shape[1], HEAD_DIM), cached),
                pl.BlockSpec((HEAD_DIM, width), lambda h, r, m: (h, 0)),
            ],
            out_specs=pl.BlockSpec((count, width), lambda h, r, m: (0, 0)),
            scratch_shapes=[pltpu.VMEM((count, width), jnp.float32)],
        ),
        cost_estimate=pl.CostEstimate(
            flops=4 * requests * here * keys * columns + 2 * count * columns * width,
            bytes_accessed=4 * requests * keys * columns + 2 * columns * width,
            transcendentals=requests * here * keys * (columns // HEAD_DIM),
        ),
        name="attention",
    )(meta, qkv, cosine, sine, tails, pk, pv, tk, tv, wo)


MLP_STEPS = 4


def mlp_body(*refs):
    t_own, t_other = refs[:2]
    ups, downs = refs[2:6], refs[6:10]
    o_own, o_other, acc_ref, hidden_ref = refs[10:]
    step = pl.program_id(0)

    @pl.when(step < MLP_STEPS)
    def _():
        rows = jnp.concatenate([t_own[...], t_other[...]], axis=0)
        term = jnp.dot(
            rows, jnp.concatenate([up[...] for up in ups], axis=1), preferred_element_type=jnp.float32
        )

        @pl.when(step == 0)
        def _():
            acc_ref[...] = term

        @pl.when(step > 0)
        def _():
            acc_ref[...] += term

    @pl.when(step == MLP_STEPS - 1)
    def _():
        hidden_ref[...] = jax.nn.gelu(acc_ref[...], approximate=True).astype(jnp.bfloat16)

    @pl.when(step >= MLP_STEPS)
    def _():
        result = jnp.dot(
            hidden_ref[...],
            jnp.concatenate([down[...] for down in downs], axis=0),
            preferred_element_type=jnp.float32,
        ).astype(jnp.bfloat16)
        half = result.shape[0] // 2
        o_own[...] = result[:half]
        o_other[...] = result[half:]


def mlp_call(t_own, t_other, ups, downs):
    count, width = t_own.shape
    units = ups[0].shape[1]
    chunk = width // MLP_STEPS
    first = lambda i: jnp.minimum(i, MLP_STEPS - 1)
    second = lambda i: jnp.maximum(i - MLP_STEPS, 0)
    rows = pl.BlockSpec((count, chunk), lambda i: (0, first(i)))
    out = pl.BlockSpec((count, chunk), lambda i: (0, second(i)))
    return pl.pallas_call(
        mlp_body,
        out_shape=[jax.ShapeDtypeStruct((count, width), jnp.bfloat16)] * 2,
        grid=(2 * MLP_STEPS,),
        in_specs=[rows, rows]
        + [pl.BlockSpec((chunk, units), lambda i: (first(i), 0))] * 4
        + [pl.BlockSpec((units, chunk), lambda i: (0, second(i)))] * 4,
        out_specs=[out, out],
        scratch_shapes=[
            pltpu.VMEM((2 * count, 4 * units), jnp.float32),
            pltpu.VMEM((2 * count, 4 * units), jnp.bfloat16),
        ],
        cost_estimate=pl.CostEstimate(
            flops=4 * 2 * count * width * 4 * units,
            bytes_accessed=2 * (4 * count * width + 8 * units * width),
            transcendentals=2 * count * 4 * units,
        ),
        name="mlp",
    )(t_own, t_other, *ups, *downs)


def shards(
    tokens,
    input_gain,
    qkv_weight,
    out_weight,
    in_weight,
    down_weight,
    final_gain,
    score_weight,
    prompt_keys,
    prompt_values,
    tail_keys,
    tail_values,
    prompt_lengths,
    tail_lengths,
):
    req_dev, samp_dev, fresh, width = tokens.shape
    own_rows = req_dev * samp_dev * fresh
    ups = [in_weight] + [from_neighbour(in_weight, axis) for axis in "xyz"]
    downs = [down_weight] + [from_neighbour(down_weight, axis) for axis in "xyz"]
    residual = tokens.astype(jnp.float32).reshape(own_rows, width)
    normed = layer_norm(residual, input_gain).astype(jnp.bfloat16)
    groups = token_groups()
    sharing = len(groups[0])
    visitors = lax.all_to_all(
        jnp.tile(normed, (sharing, 1)), AXES, 0, 0, axis_index_groups=groups, tiled=True
    )

    rows = normed
    for axis in HID:
        rows = jnp.concatenate([rows, swap(rows, axis)], axis=0)
    qkv = qkv_call(rows, jnp.transpose(qkv_weight, (1, 0, 2)))
    positions = (
        prompt_lengths[:, None, None]
        + tail_lengths[:, :, None]
        + jnp.arange(fresh, dtype=jnp.int32)[None, None, :]
    )
    samples = tail_lengths.shape[1]
    cosine, sine = rotation_tables(positions.reshape(req_dev, samples * fresh))
    tails = jnp.repeat(tail_lengths, fresh, axis=1)[:, :, None]
    meta = jnp.concatenate([prompt_lengths, lax.axis_index(HID).astype(jnp.int32)[None]])
    slab = tail_keys.shape[-1]
    partial = attention_call(
        meta,
        qkv,
        cosine,
        sine,
        tails,
        prompt_keys,
        prompt_values,
        tail_keys.reshape(req_dev, -1, slab),
        tail_values.reshape(req_dev, -1, slab),
        out_weight,
    )
    for axis in reversed(HID):
        half = partial.shape[0] // 2
        partial = partial[:half].astype(jnp.float32) + swap(partial[half:], axis).astype(jnp.float32)
        if axis != HID[0]:
            partial = partial.astype(jnp.bfloat16)

    mine, others = mlp_call(visitors, swap(visitors, "c"), ups, downs)
    summed = mine.astype(jnp.float32) + swap(others, "c").astype(jnp.float32)
    returned = lax.all_to_all(
        summed.astype(jnp.bfloat16), AXES, 0, 0, axis_index_groups=groups, tiled=True
    )
    feed_forward = jnp.sum(
        returned.reshape(sharing, own_rows, width).astype(jnp.float32), axis=0
    )

    final_state = residual + partial + feed_forward
    next_hidden = final_state.astype(jnp.bfloat16).reshape(req_dev, samp_dev, fresh, width)
    sample_scores = jnp.sum(
        layer_norm(final_state, final_gain) * score_weight.astype(jnp.float32), axis=-1
    )
    return (next_hidden, sample_scores.reshape(req_dev, samp_dev, fresh))


def solution(mesh):
    grid = Mesh(mesh.devices.reshape(SIDE, SIDE, 2, 2, CORES), AXES)
    placed = (
        P(REQ, HID, None, None),
        P(),
        P(None, None, HID),
        P(HID, None),
        P(None, REQ + HID),
        P(REQ + HID, None),
        P(),
        P(),
        P(REQ, None, HID),
        P(REQ, None, HID),
        P(REQ, None, None, HID),
        P(REQ, None, None, HID),
        P(REQ),
        P(REQ, None),
    )
    return jax.shard_map(
        shards,
        mesh=grid,
        in_specs=placed,
        out_specs=(P(REQ, HID, None, None), P(REQ, HID, None)),
        check_vma=False,
    )
```

time: 823 us -> 117 us (0.14)
  waiting for transfers between devices: 735 us -> 35.7 us
  matrix products: 38.6 us -> 0 us
  starting transfers between devices: 0.12 us -> 33 us
  Pallas kernels: 0 us -> 30.6 us
  local copies, waits for them, and re-layouts: 26.3 us -> 7.03 us
  between operations: 14.1 us -> 0.88 us
    reduce_scatter x2 -> x0, waiting for transfers between devices: 680 us -> none  [the longest x1 667 us: shards(): lax.psum_scatter(jnp.dot(hidden_units, down_weight, preferred_element_typ...]
    all_gather x1 -> x0, waiting for transfers between devices: 55.2 us -> none  [shards(): gathered = lax.all_gather(normed, ('req', 'hid'), axis=0, tiled=True)]
    dot_general x9 -> x0, matrix products: 38.6 us -> none  [the longest x1 14.4 us: shards(): jnp.dot(hidden_units, down_weight, preferred_element_type=jnp.float32)]
    pallas_call x0 -> x3, Pallas kernels: none -> 30.6 us  [the longest x1 13.3 us: attention_call(): pl.pallas_call(attention_body, out_shape=jax.ShapeDtypeStruct((count, wid...]
    ppermute x0 -> x14, starting transfers between devices: none -> 19.5 us  [the longest x8 13.4 us: swap(): return lax.ppermute(values, axis, [(0, 1), (1, 0)])]
    ppermute x0 -> x14, waiting for transfers between devices: none -> 18.4 us  [the longest x8 18.4 us: swap(): return lax.ppermute(values, axis, [(0, 1), (1, 0)])]
    unnamed x13 -> x14, local copies, waits for them, and re-layouts: 17.6 us -> 0.03 us
    all_to_all x0 -> x2, waiting for transfers between devices: none -> 17.3 us  [the longest x1 17.3 us: shards(): lax.all_to_all(summed.astype(jnp.bfloat16), AXES, 0, 0, axis_index_groups...]
  transfers between devices with their start and end apart: 3 -> 16, of which waited for: 3 -> 3; matrix products, arithmetic and copies ran while one was open for 4% -> 8% of each run, Pallas kernels for 0% -> 27%
where the time goes in v1:
time: 117 us; the launch traced here: 115 us
  waiting for transfers between devices  35.7 us (31%)
  starting transfers between devices  33 us (28%)
  Pallas kernels  30.6 us (26%)
  other arithmetic  8.02 us (7%)
  local copies, waits for them, and re-layouts  7.03 us (6%)
    ppermute x8, waiting for transfers between devices, swap(): return lax.ppermute(values, axis, [(0, 1), (1, 0)])  18.4 us
    all_to_all x1, waiting for transfers between devices, shards(): lax.all_to_all(summed.astype(jnp.bfloat16), AXES, 0, 0, axis_index_groups...  17.3 us
    ppermute x8, starting transfers between devices, swap(): return lax.ppermute(values, axis, [(0, 1), (1, 0)])  13.4 us
    pallas_call x1, Pallas kernels, attention_call(): pl.pallas_call(attention_body, out_shape=jax.ShapeDtypeStruct((count, wid...  13.3 us
    pallas_call x1, Pallas kernels, mlp_call(): pl.pallas_call(mlp_body, out_shape=[jax.ShapeDtypeStruct((count, width),...  9.29 us
    pallas_call x1, Pallas kernels, qkv_call(): pl.pallas_call(qkv_body, out_shape=jax.ShapeDtypeStruct((triple, count, c...  7.97 us
    all_to_all x1, starting transfers between devices, shards(): lax.all_to_all(jnp.tile(normed, (sharing, 1)), AXES, 0, 0, axis_index_gro...  7.04 us
    all_to_all x1, starting transfers between devices, shards(): lax.all_to_all(summed.astype(jnp.bfloat16), AXES, 0, 0, axis_index_groups...  6.53 us
  transfers between devices with their start and end apart: 16, of which 3 were waited for; matrix products, arithmetic and copies ran while one was open for 8% of the time, Pallas kernels for 27%

profile of v1, /device:TPU:0, one launch (start us, length us, event | category | flops | bytes accessed | tf_op | source)
XLA Modules:
  0.0 115.3 jit_solution(1169598032330623362)
XLA Ops:
  0.6 0.0 copy-start.2
  0.7 0.9 reshape.157
  1.6 1.0 convert_reduce_fusion.1
  2.6 1.1 multiply_reduce_fusion.2
  3.7 0.1 div.15
  3.8 0.1 rsqrt.20
  3.9 0.8 multiply_convert_fusion
  4.7 4.0 %collective-permute-start = (bf16[8,4096]{1,0:T(8,128)(2,1)S(1)}, bf16[8,4096]{1,0:T(8,128)(2,1)S(1)}, u32[]{:S(2)}, u32[]{:S(2)}) collective-permute-start(bf16[8,4096]{1,0:T(8,128)(2,1)S(1)} %multiply_convert_fusion), channel_id=1, source_target_pairs={{0,4},{4,0},{1,5},{5,1},{2,6},{6,2},{3,7},{7,3},{8,12},{12,8},{9,1... | collective-permute-start | bytes 196616 | tf_op jit(solution)/shard_map/ppermute | solution.py:50
  8.7 1.5 %collective-permute-start.7 = (bf16[4096,128]{1,0:T(8,128)(2,1)}, bf16[4096,128]{1,0:T(8,128)(2,1)}, u32[]{:S(2)}, u32[]{:S(2)}) collective-permute-start(bf16[4096,128]{1,0:T(8,128)(2,1)} %refs_2_.1), channel_id=1, source_target_pairs={{0,8},{1,25},{2,10},{3,27},{4,12},{5,29},{6,14},{7,31},{8,16},{9,1... | collective-permute-start | bytes 3145736 | tf_op jit(solution)/shard_map/ppermute | solution.py:46
  10.2 1.6 %collective-permute-start.8 = (bf16[4096,128]{1,0:T(8,128)(2,1)}, bf16[4096,128]{1,0:T(8,128)(2,1)}, u32[]{:S(2)}, u32[]{:S(2)}) collective-permute-start(bf16[4096,128]{1,0:T(8,128)(2,1)} %refs_2_.1), channel_id=1, source_target_pairs={{0,32},{1,97},{2,34},{3,99},{4,36},{5,101},{6,38},{7,103},{8,40},{... | collective-permute-start | bytes 3145736 | tf_op jit(solution)/shard_map/ppermute | solution.py:46
  11.8 1.0 collective-permute-start.9
  12.8 1.1 tile.2
  13.9 7.0 %all-to-all-start = ((bf16[16,8,4096]{2,1,0:T(8,128)(2,1)}), bf16[16,8,4096]{2,1,0:T(8,128)(2,1)S(1)}, u32[]{:S(2)}, u32[]{:S(2)}) async-start(bf16[16,8,4096]{2,1,0:T(8,128)(2,1)} %tile.2), calls=%async_computation | async-start | bytes 2097152 | tf_op jit(solution)/shard_map/all_to_all | solution.py:313
  21.0 0.1 collective-permute-start.10
  21.0 0.0 collective-permute-done
  21.1 2.0 %collective-permute-start.1 = (bf16[16,4096]{1,0:T(8,128)(2,1)S(1)}, bf16[16,4096]{1,0:T(8,128)(2,1)S(1)}, u32[]{:S(2)}, u32[]{:S(2)}) collective-permute-start(bf16[16,4096]{1,0:T(8,128)(2,1)S(1)} %pad_maximum_fusion.2), channel_id=1, source_target_pairs={{0,2},{2,0},{1,3},{3,1},{4,6},{6,4},{5,7},{7,5},{8,10},{10,8},{9,1... | collective-permute-start | bytes 393224 | tf_op jit(solution)/shard_map/ppermute | solution.py:50
  23.1 0.1 broadcast_add_fusion
  23.1 16.3 %collective-permute-done.1 = bf16[16,4096]{1,0:T(8,128)(2,1)S(1)} collective-permute-done((bf16[16,4096]{1,0:T(8,128)(2,1)S(1)}, bf16[16,4096]{1,0:T(8,128)(2,1)S(1)}, u32[]{:S(2)}, u32[]{:S(2)}) %collective-permute-start.1) | collective-permute-done | bytes 131104 | tf_op jit(solution)/shard_map/ppermute | solution.py:50
  39.5 2.4 %collective-permute-start.2 = (bf16[32,4096]{1,0:T(8,128)(2,1)S(1)}, bf16[32,4096]{1,0:T(8,128)(2,1)S(1)}, u32[]{:S(2)}, u32[]{:S(2)}) collective-permute-start(bf16[32,4096]{1,0:T(8,128)(2,1)S(1)} %pad_maximum_fusion.1), channel_id=1, source_target_pairs={{0,1},{1,0},{2,3},{3,2},{4,5},{5,4},{6,7},{7,6},{8,9},{9,8},{10,11... | collective-permute-start | bytes 786440 | tf_op jit(solution)/shard_map/ppermute | solution.py:50
  41.9 0.1 broadcast_in_dim.15
  42.0 0.1 mul.100
  42.1 0.1 add.93
  42.2 0.1 add.94
  42.3 0.1 add.96
  42.3 0.1 broadcast_in_dim.18
  42.4 0.7 broadcast_in_dim_reshape.5.tails_ref
  43.1 0.0 collective-permute-done.2
  43.1 0.0 collective-permute-start.11
  43.1 0.0 collective-permute-done.7.refs_3_
  43.1 1.9 %collective-permute-start.12 = (bf16[128,4096]{1,0:T(8,128)(2,1)S(1)}, bf16[128,4096]{1,0:T(8,128)(2,1)}, u32[]{:S(2)}, u32[]{:S(2)}) collective-permute-start(bf16[128,4096]{1,0:T(8,128)(2,1)S(1)} %copy-done.2), channel_id=1, source_target_pairs={{0,2},{1,7},{2,4},{3,1},{4,6},{5,3},{6,0},{7,5},{8,10},{9,15},{10,... | collective-permute-start | bytes 3145736 | tf_op jit(solution)/shard_map/ppermute | solution.py:46
  45.1 0.0 all-to-all-done
  45.1 0.0 collective-permute-done.8.refs_4_
  45.1 0.1 collective-permute-start.6
  45.2 0.2 fusion.1
  45.4 0.7 pad.8.cos_ref
  46.0 0.6 pad.9.sin_ref
  46.7 0.7 pad_add_fusion.meta_ref
  47.3 0.9 pad_maximum_fusion.rows_ref
  48.2 8.0 %qkv.1.qkv_ref = bf16[3,64,512]{2,1,0:T(8,128)(2,1)} custom-call(bf16[64,4096]{1,0:T(8,128)(2,1)} %pad_maximum_fusion.rows_ref, bf16[3,4096,512]{2,1,0:T(8,128)(2,1)} %bitcast.7), custom_call_target="tpu_custom_call" | custom-call | flops 805306368 | bytes 12582912 | tf_op jit(solution)/shard_map/qkv/pallas_call | solution.py:81
  56.2 13.3 %attention.1 = bf16[64,4096]{1,0:T(8,128)(2,1)} custom-call(s32[3]{0:T(128)} %pad_add_fusion.meta_ref, bf16[3,64,512]{2,1,0:T(8,128)(2,1)} %qkv.1.qkv_ref, f32[2,32,256]{2,1,0:T(8,128)} %pad.8.cos_ref, f32[2,32,256]{2,1,0:T(8,128)} %pad.9.sin_ref, s32[2,32,1]{2,1,0:T(8,128)} %broadcast_in_dim_reshape.5.tails_ref, bf16[2,2048,512]{2,1,0:T(8,128)(2,1)} %pk_ref.1, ...), custom_call_target="tpu_custom_call" | custom-call | flops 671088640 | bytes 16777216 | tf_op jit(solution)/shard_map/attention/pallas_call | solution.py:191
  69.5 1.0 slice.25
  70.4 0.0 collective-permute-done.9.refs_5_
  70.4 0.5 collective-permute-start.3
  71.0 0.0 collective-permute-done.10.refs_7_
  71.0 0.0 collective-permute-done.11.refs_8_
  71.0 0.0 collective-permute-done.6.refs_1_
  71.0 9.3 %mlp.1 = (bf16[128,4096]{1,0:T(8,128)(2,1)}, bf16[128,4096]{1,0:T(8,128)(2,1)}) custom-call(bf16[128,4096]{1,0:T(8,128)(2,1)} %bitcast.9, bf16[128,4096]{1,0:T(8,128)(2,1)} %collective-permute-done.6.refs_1_, bf16[4096,128]{1,0:T(8,128)(2,1)} %refs_2_.1, bf16[4096,128]{1,0:T(8,128)(2,1)} %collective-permute-done.7.refs_3_, ...), custom_call_target="tpu_custom_call" | custom-call | flops 2147483648 | bytes 12582912 | tf_op jit(solution)/shard_map/mlp/pallas_call | solution.py:268
  80.3 0.1 collective-permute-start.13
  80.4 0.0 collective-permute-done.3
  80.4 0.1 add_convert_fusion.1
  80.5 0.6 collective-permute-start.4
  81.1 2.1 %collective-permute-done.13 = bf16[128,4096]{1,0:T(8,128)(2,1)S(1)} collective-permute-done((bf16[128,4096]{1,0:T(8,128)(2,1)}, bf16[128,4096]{1,0:T(8,128)(2,1)S(1)}, u32[]{:S(2)}, u32[]{:S(2)}) %collective-permute-start.13) | collective-permute-done | bytes 1048608 | tf_op jit(solution)/shard_map/ppermute | solution.py:50
  83.3 2.5 %fusion = bf16[16,8,4096]{2,1,0:T(8,128)(2,1)} fusion(bf16[128,4096]{1,0:T(8,128)(2,1)S(1)} %collective-permute-done.13, bf16[128,4096]{1,0:T(8,128)(2,1)} %get-tuple-element.4), kind=kLoop, calls=%fused_computation.2 | loop fusion | flops 2097152 | bytes 3145728 | tf_op jit(solution)/shard_map/all_to_all | solution.py:351
  85.7 6.5 %all-to-all-start.1 = ((bf16[16,8,4096]{2,1,0:T(8,128)(2,1)}), bf16[16,8,4096]{2,1,0:T(8,128)(2,1)S(1)}, u32[]{:S(2)}, u32[]{:S(2)}) async-start(bf16[16,8,4096]{2,1,0:T(8,128)(2,1)} %fusion), calls=%async_computation.1 | async-start | bytes 2097152 | tf_op jit(solution)/shard_map/all_to_all | solution.py:351
  92.3 0.0 collective-permute-done.4
  92.3 3.5 %collective-permute-start.5 = (bf16[8,4096]{1,0:T(8,128)(2,1)S(1)}, bf16[8,4096]{1,0:T(8,128)(2,1)S(1)}, u32[]{:S(2)}, u32[]{:S(2)}) collective-permute-start(bf16[8,4096]{1,0:T(8,128)(2,1)S(1)} %slice.29), channel_id=1, source_target_pairs={{0,4},{4,0},{1,5},{5,1},{2,6},{6,2},{3,7},{7,3},{8,12},{12,8},{9,1... | collective-permute-start | bytes 196616 | tf_op jit(solution)/shard_map/ppermute | solution.py:50
  95.9 17.3 %all-to-all-done.1 = bf16[16,8,4096]{2,1,0:T(8,128)(2,1)S(1)} async-done(((bf16[16,8,4096]{2,1,0:T(8,128)(2,1)}), bf16[16,8,4096]{2,1,0:T(8,128)(2,1)S(1)}, u32[]{:S(2)}, u32[]{:S(2)}) %all-to-all-start.1) | async-done | bytes 1048608 | tf_op jit(solution)/shard_map/all_to_all | solution.py:351
  113.2 0.1 convert_reduce_fusion
  113.3 0.0 collective-permute-done.5
  113.3 0.2 fusion.2
  113.5 0.2 multiply_reduce_fusion.1
  113.7 0.2 multiply_reduce_fusion
  113.9 0.7 reshape.160
  114.6 0.7 reshape.161
  (28 shorter events, 0.2 us)
Async XLA Ops:
  0.6 20.3 %copy-start.2 = (bf16[128,4096]{1,0:T(8,128)(2,1)S(1)}, bf16[128,4096]{1,0:T(8,128)(2,1)}, u32[]{:S(2)}) copy-start(bf16[128,4096]{1,0:T(8,128)(2,1)} %refs_6_.1) | copy-start | bytes 3145732
  0.6 22.4 %copy-start.6 = (s32[2]{0:T(128)S(1)}, s32[2]{0:T(128)}, u32[]{:S(2)}) copy-start(s32[2]{0:T(128)} %param.26) | copy-start | bytes 28
  0.7 22.4 %copy-start.5 = (s32[2,16]{1,0:T(2,128)S(1)}, s32[2,16]{1,0:T(2,128)}, u32[]{:S(2)}) copy-start(s32[2,16]{1,0:T(2,128)} %param.27) | copy-start | bytes 388
  4.7 16.4 %collective-permute-start = (bf16[8,4096]{1,0:T(8,128)(2,1)S(1)}, bf16[8,4096]{1,0:T(8,128)(2,1)S(1)}, u32[]{:S(2)}, u32[]{:S(2)}) collective-permute-start(bf16[8,4096]{1,0:T(8,128)(2,1)S(1)} %multiply_convert_fusion), channel_id=1, source_target_pairs={{0,4},{4,0},{1,5},{5,1},{2,6},{6,2},{3,7},{7,3},{8,12},{12,8},{9,1... | collective-permute-start | bytes 196616 | tf_op jit(solution)/shard_map/ppermute | solution.py:50
  8.7 34.4 %collective-permute-start.7 = (bf16[4096,128]{1,0:T(8,128)(2,1)}, bf16[4096,128]{1,0:T(8,128)(2,1)}, u32[]{:S(2)}, u32[]{:S(2)}) collective-permute-start(bf16[4096,128]{1,0:T(8,128)(2,1)} %refs_2_.1), channel_id=1, source_target_pairs={{0,8},{1,25},{2,10},{3,27},{4,12},{5,29},{6,14},{7,31},{8,16},{9,1... | collective-permute-start | bytes 3145736 | tf_op jit(solution)/shard_map/ppermute | solution.py:46
  10.2 34.9 %collective-permute-start.8 = (bf16[4096,128]{1,0:T(8,128)(2,1)}, bf16[4096,128]{1,0:T(8,128)(2,1)}, u32[]{:S(2)}, u32[]{:S(2)}) collective-permute-start(bf16[4096,128]{1,0:T(8,128)(2,1)} %refs_2_.1), channel_id=1, source_target_pairs={{0,32},{1,97},{2,34},{3,99},{4,36},{5,101},{6,38},{7,103},{8,40},{... | collective-permute-start | bytes 3145736 | tf_op jit(solution)/shard_map/ppermute | solution.py:46
  11.8 58.7 %collective-permute-start.9 = (bf16[4096,128]{1,0:T(8,128)(2,1)}, bf16[4096,128]{1,0:T(8,128)(2,1)}, u32[]{:S(2)}, u32[]{:S(2)}) collective-permute-start(bf16[4096,128]{1,0:T(8,128)(2,1)} %refs_2_.1), channel_id=1, source_target_pairs={{0,2},{1,7},{2,4},{3,1},{4,6},{5,3},{6,0},{7,5},{8,10},{9,15},{10,... | collective-permute-start | bytes 3145736 | tf_op jit(solution)/shard_map/ppermute | solution.py:46
  13.9 31.2 %all-to-all-start = ((bf16[16,8,4096]{2,1,0:T(8,128)(2,1)}), bf16[16,8,4096]{2,1,0:T(8,128)(2,1)S(1)}, u32[]{:S(2)}, u32[]{:S(2)}) async-start(bf16[16,8,4096]{2,1,0:T(8,128)(2,1)} %tile.2), calls=%async_computation | async-start | bytes 2097152 | tf_op jit(solution)/shard_map/all_to_all | solution.py:313
  21.0 50.0 %collective-permute-start.10 = (bf16[128,4096]{1,0:T(8,128)(2,1)S(1)}, bf16[128,4096]{1,0:T(8,128)(2,1)}, u32[]{:S(2)}, u32[]{:S(2)}) collective-permute-start(bf16[128,4096]{1,0:T(8,128)(2,1)S(1)} %copy-done.2), channel_id=1, source_target_pairs={{0,8},{1,25},{2,10},{3,27},{4,12},{5,29},{6,14},{7,31},{8,16},{9,1... | collective-permute-start | bytes 3145736 | tf_op jit(solution)/shard_map/ppermute | solution.py:46
  21.1 18.4 %collective-permute-start.1 = (bf16[16,4096]{1,0:T(8,128)(2,1)S(1)}, bf16[16,4096]{1,0:T(8,128)(2,1)S(1)}, u32[]{:S(2)}, u32[]{:S(2)}) collective-permute-start(bf16[16,4096]{1,0:T(8,128)(2,1)S(1)} %pad_maximum_fusion.2), channel_id=1, source_target_pairs={{0,2},{2,0},{1,3},{3,1},{4,6},{6,4},{5,7},{7,5},{8,10},{10,8},{9,1... | collective-permute-start | bytes 393224 | tf_op jit(solution)/shard_map/ppermute | solution.py:50
  39.5 3.6 %collective-permute-start.2 = (bf16[32,4096]{1,0:T(8,128)(2,1)S(1)}, bf16[32,4096]{1,0:T(8,128)(2,1)S(1)}, u32[]{:S(2)}, u32[]{:S(2)}) collective-permute-start(bf16[32,4096]{1,0:T(8,128)(2,1)S(1)} %pad_maximum_fusion.1), channel_id=1, source_target_pairs={{0,1},{1,0},{2,3},{3,2},{4,5},{5,4},{6,7},{7,6},{8,9},{9,8},{10,11... | collective-permute-start | bytes 786440 | tf_op jit(solution)/shard_map/ppermute | solution.py:50
  43.1 27.9 %collective-permute-start.11 = (bf16[128,4096]{1,0:T(8,128)(2,1)S(1)}, bf16[128,4096]{1,0:T(8,128)(2,1)}, u32[]{:S(2)}, u32[]{:S(2)}) collective-permute-start(bf16[128,4096]{1,0:T(8,128)(2,1)S(1)} %copy-done.2), channel_id=1, source_target_pairs={{0,32},{1,97},{2,34},{3,99},{4,36},{5,101},{6,38},{7,103},{8,40},{... | collective-permute-start | bytes 3145736 | tf_op jit(solution)/shard_map/ppermute | solution.py:46
  43.1 27.9 %collective-permute-start.12 = (bf16[128,4096]{1,0:T(8,128)(2,1)S(1)}, bf16[128,4096]{1,0:T(8,128)(2,1)}, u32[]{:S(2)}, u32[]{:S(2)}) collective-permute-start(bf16[128,4096]{1,0:T(8,128)(2,1)S(1)} %copy-done.2), channel_id=1, source_target_pairs={{0,2},{1,7},{2,4},{3,1},{4,6},{5,3},{6,0},{7,5},{8,10},{9,15},{10,... | collective-permute-start | bytes 3145736 | tf_op jit(solution)/shard_map/ppermute | solution.py:46
  45.1 11.1 %copy-start = (bf16[16,8,4096]{2,1,0:T(8,128)(2,1)}, bf16[16,8,4096]{2,1,0:T(8,128)(2,1)S(1)}, u32[]{:S(2)}) copy-start(bf16[16,8,4096]{2,1,0:T(8,128)(2,1)S(1)} %all-to-all-done) | copy-start | bytes 3145732
  45.1 25.9 %collective-permute-start.6 = (bf16[128,4096]{1,0:T(8,128)(2,1)S(1)}, bf16[128,4096]{1,0:T(8,128)(2,1)}, u32[]{:S(2)}, u32[]{:S(2)}) collective-permute-start(bf16[128,4096]{1,0:T(8,128)(2,1)S(1)} %bitcast.8), channel_id=1, source_target_pairs={{0,1},{1,0},{2,3},{3,2},{4,5},{5,4},{6,7},{7,6},{8,9},{9,8},{10,11... | collective-permute-start | bytes 3145736 | tf_op jit(solution)/shard_map/ppermute | solution.py:50
  70.4 10.0 %copy-start.1 = (bf16[64,4096]{1,0:T(8,128)(2,1)S(1)}, bf16[64,4096]{1,0:T(8,128)(2,1)}, u32[]{:S(2)}) copy-start(bf16[64,4096]{1,0:T(8,128)(2,1)} %attention.1) | copy-start | bytes 1572868
  70.4 10.0 %collective-permute-start.3 = (bf16[32,4096]{1,0:T(8,128)(2,1)S(1)}, bf16[32,4096]{1,0:T(8,128)(2,1)S(1)}, u32[]{:S(2)}, u32[]{:S(2)}) collective-permute-start(bf16[32,4096]{1,0:T(8,128)(2,1)S(1)} %slice.25), channel_id=1, source_target_pairs={{0,1},{1,0},{2,3},{3,2},{4,5},{5,4},{6,7},{7,6},{8,9},{9,8},{10,11... | collective-permute-start | bytes 786440 | tf_op jit(solution)/shard_map/ppermute | solution.py:50
  80.3 2.9 %collective-permute-start.13 = (bf16[128,4096]{1,0:T(8,128)(2,1)}, bf16[128,4096]{1,0:T(8,128)(2,1)S(1)}, u32[]{:S(2)}, u32[]{:S(2)}) collective-permute-start(bf16[128,4096]{1,0:T(8,128)(2,1)} %get-tuple-element.5), channel_id=1, source_target_pairs={{0,1},{1,0},{2,3},{3,2},{4,5},{5,4},{6,7},{7,6},{8,9},{9,8},{10,11... | collective-permute-start | bytes 3145736 | tf_op jit(solution)/shard_map/ppermute | solution.py:50
  80.5 11.8 %collective-permute-start.4 = (bf16[16,4096]{1,0:T(8,128)(2,1)S(1)}, bf16[16,4096]{1,0:T(8,128)(2,1)S(1)}, u32[]{:S(2)}, u32[]{:S(2)}) collective-permute-start(bf16[16,4096]{1,0:T(8,128)(2,1)S(1)} %slice.27), channel_id=1, source_target_pairs={{0,2},{2,0},{1,3},{3,1},{4,6},{6,4},{5,7},{7,5},{8,10},{10,8},{9,1... | collective-permute-start | bytes 393224 | tf_op jit(solution)/shard_map/ppermute | solution.py:50
  83.3 9.0 %copy-start.4 = (bf16[4096]{0:T(1024)(128)(2,1)S(1)}, bf16[4096]{0:T(1024)(128)(2,1)}, u32[]{:S(2)}) copy-start(bf16[4096]{0:T(1024)(128)(2,1)} %param.21) | copy-start | bytes 24580
  85.7 28.0 %copy-start.3 = (f32[4096]{0:T(1024)S(1)}, f32[4096]{0:T(1024)}, u32[]{:S(2)}) copy-start(f32[4096]{0:T(1024)} %param.20) | copy-start | bytes 49156
  85.7 27.4 %all-to-all-start.1 = ((bf16[16,8,4096]{2,1,0:T(8,128)(2,1)}), bf16[16,8,4096]{2,1,0:T(8,128)(2,1)S(1)}, u32[]{:S(2)}, u32[]{:S(2)}) async-start(bf16[16,8,4096]{2,1,0:T(8,128)(2,1)} %fusion), calls=%async_computation.1 | async-start | bytes 2097152 | tf_op jit(solution)/shard_map/all_to_all | solution.py:351
  92.3 21.0 %collective-permute-start.5 = (bf16[8,4096]{1,0:T(8,128)(2,1)S(1)}, bf16[8,4096]{1,0:T(8,128)(2,1)S(1)}, u32[]{:S(2)}, u32[]{:S(2)}) collective-permute-start(bf16[8,4096]{1,0:T(8,128)(2,1)S(1)} %slice.29), channel_id=1, source_target_pairs={{0,4},{4,0},{1,5},{5,1},{2,6},{6,2},{3,7},{7,3},{8,12},{12,8},{9,1... | collective-permute-start | bytes 196616 | tf_op jit(solution)/shard_map/ppermute | solution.py:50

commit v2 on v0

v2 whole, which is shorter than its diff:
```python
import jax
import jax.numpy as jnp
from jax import lax
from jax.experimental import pallas as pl
from jax.experimental.pallas import tpu as pltpu
from jax.sharding import Mesh
from jax.sharding import PartitionSpec as P

HEAD_DIM = 256
ROT = 64
LANES = 128
VERY_LOW = -1e30
CUT = 2
MIB = 2**20
SMEM = pl.BlockSpec(memory_space=pltpu.SMEM)
VMEM = pl.BlockSpec(memory_space=pltpu.VMEM)
HBM = pl.BlockSpec(memory_space=pltpu.HBM)
SIDE = 4
CORES = 2
AXES = ("y", "x", "u", "w", "c")
REQ = ("y", "x")
HID = ("u", "w", "c")


def device_at(y, x, z, core):
    return (((y % SIDE) * SIDE + x % SIDE) * SIDE + z % SIDE) * CORES + core


def places():
    for y in range(SIDE):
        for x in range(SIDE):
            for z in range(SIDE):
                for core in range(CORES):
                    yield y, x, z, core


def token_groups():
    groups = {}
    for y, x, z, core in places():
        groups.setdefault(((x + z) % 2, (y + z) % 2, core), []).append(device_at(y, x, z, core))
    return [sorted(group) for group in groups.values()]


def from_neighbour(values, axis):
    moves = []
    for y, x, z, core in places():
        step = 1 - 2 * core
        target = device_at(
            y + step * (axis == "y"), x + step * (axis == "x"), z + step * (axis == "z"), core
        )
        moves.append((device_at(y, x, z, core), target))
    return lax.ppermute(values, AXES, moves)


def swap(values, *axes):
    last = 2 ** len(axes) - 1
    return lax.ppermute(values, axes, [(i, last - i) for i in range(last + 1)])


def normalised(values, gain):
    centred = values - jnp.mean(values, axis=1, keepdims=True)
    spread = jnp.mean(centred * centred, axis=1, keepdims=True)
    return centred * lax.rsqrt(spread + 1e-05) * gain


def start_body(
    tokens_hbm, gain_hbm, up_hbm, down_hbm, normed_ref, copies_ref, packed_hbm, tokens_ref, gain_ref, rows, packed, down_ref, sem, out_sem
):
    requests, samples, fresh, width = tokens_ref.shape
    blocks = up_hbm.shape[0]
    upper, lower = pl.ds(0, blocks), pl.ds(blocks, blocks)
    inward = [
        pltpu.make_async_copy(down_hbm, down_ref, sem.at[0]),
        pltpu.make_async_copy(up_hbm, packed.at[upper], sem.at[1]),
        pltpu.make_async_copy(tokens_hbm, tokens_ref, sem.at[2]),
        pltpu.make_async_copy(gain_hbm, gain_ref, sem.at[3]),
    ]
    outward = [
        pltpu.make_async_copy(packed.at[lower], packed_hbm.at[lower], out_sem.at[0]),
        pltpu.make_async_copy(packed.at[upper], packed_hbm.at[upper], out_sem.at[1]),
    ]
    for copy in inward:
        copy.start()
    inward[0].wait()
    for j in range(blocks):
        packed[blocks + j] = down_ref[:, j * LANES : (j + 1) * LANES]
    outward[0].start()
    inward[1].wait()
    outward[1].start()
    inward[2].wait()
    inward[3].wait()
    for r in range(requests):
        for s in range(samples):
            at = (r * samples + s) * fresh
            rows[at : at + fresh] = tokens_ref[r, s].astype(jnp.float32)
    normed = normalised(rows[...], gain_ref[...]).astype(jnp.bfloat16)
    normed_ref[...] = normed
    for i in range(copies_ref.shape[0]):
        copies_ref[i] = normed
    for copy in outward:
        copy.wait()


def start_call(tokens, gain, up, down, sharing):
    requests, samples, fresh, width = tokens.shape
    own_rows = requests * samples * fresh
    blocks = width // LANES
    return pl.pallas_call(
        start_body,
        out_shape=[
            jax.ShapeDtypeStruct((own_rows, width), jnp.bfloat16),
            jax.ShapeDtypeStruct((sharing, own_rows, width), jnp.bfloat16),
            jax.ShapeDtypeStruct((2 * blocks, LANES, LANES), jnp.bfloat16),
        ],
        in_specs=[HBM] * 4,
        out_specs=[VMEM, VMEM, HBM],
        scratch_shapes=[
            pltpu.VMEM(tokens.shape, jnp.bfloat16),
            pltpu.VMEM((1, width), jnp.float32),
            pltpu.VMEM((own_rows, width), jnp.float32),
            pltpu.VMEM((2 * blocks, LANES, LANES), jnp.bfloat16),
            pltpu.VMEM(down.shape, jnp.bfloat16),
            pltpu.SemaphoreType.DMA((4,)),
            pltpu.SemaphoreType.DMA((2,)),
        ],
        compiler_params=pltpu.CompilerParams(vmem_limit_bytes=60 * MIB),
        name="start",
    )(tokens, gain.reshape(1, width), up.reshape(blocks, LANES, LANES), down)


def iotas(shape):
    return lax.broadcasted_iota(jnp.int32, shape, 0), lax.broadcasted_iota(jnp.int32, shape, 1)

def mixer_body(
    plen_ref, tlen_ref, hid_ref, near_ref, far_ref, turn_ref, wq_hbm, pk_hbm, pv_hbm, tk_hbm, tv_hbm, wo_hbm,
    out_ref, wq, pk, pv, tk, tv, wo, wq_sem, cache_sem, wo_sem
):
    parts, width, columns = wq.shape
    requests, prompt_len, _ = pk.shape
    samples = tlen_ref.shape[1]
    tail_len = tk.shape[1] // samples
    count = near_ref.shape[0] + far_ref.shape[0]
    here = count // requests
    fresh = here // samples
    heads = columns // HEAD_DIM
    slab = width // CUT
    def wq_copy(t, k):
        rows = pl.ds(k * slab, slab)
        return pltpu.make_async_copy(wq_hbm.at[t, rows], wq.at[t, rows], wq_sem.at[t, k])
    caches = ((pk_hbm, pk), (tk_hbm, tk), (pv_hbm, pv), (tv_hbm, tv))
    def cache_copy(r, i):
        source, target = caches[i]
        return pltpu.make_async_copy(source.at[r], target.at[r], cache_sem.at[r, i])
    def wo_copy(h):
        rows = pl.ds(h * HEAD_DIM, HEAD_DIM)
        return pltpu.make_async_copy(wo_hbm.at[rows], wo.at[rows], wo_sem.at[h])
    for t in range(parts):
        for k in range(CUT):
            wq_copy(t, k).start()
    for r in range(requests):
        for i in range(len(caches)):
            cache_copy(r, i).start()
    for h in range(heads):
        wo_copy(h).start()

    rows = jnp.concatenate([near_ref[...], far_ref[...]], axis=0)
    mixed = []
    for t in range(parts):
        acc = None
        for k in range(CUT):
            wq_copy(t, k).wait()
            term = jnp.dot(
                rows[:, k * slab : (k + 1) * slab], wq[t, k * slab : (k + 1) * slab], preferred_element_type=jnp.float32
            )
            acc = term if acc is None else acc + term
        mixed.append(acc.astype(jnp.bfloat16))

    row, col = iotas((count, count))
    block = col >> 3
    owner = hid_ref[0] ^ (((block & 1) << 2) | (block & 2) | (block >> 2))
    pick = (((col >> 2) & 1) == row // here) & (owner == ((row % here) >> 2)) & ((col & 3) == (row & 3))
    pick = jnp.where(pick, 1.0, 0.0).astype(jnp.bfloat16)
    ordered = [jnp.dot(pick, part, preferred_element_type=jnp.float32) for part in mixed]
    _, lane = iotas((count, LANES))
    even = lane % 2 == 0
    cosine, sine = turn_ref[0], turn_ref[1]

    def turned(values, h):
        head = values[:, h * HEAD_DIM : h * HEAD_DIM + LANES]
        other = jnp.where(even, pltpu.roll(head, LANES - 1, 1), pltpu.roll(head, 1, 1))
        rest = values[:, h * HEAD_DIM + LANES : (h + 1) * HEAD_DIM]
        return jnp.concatenate([head * cosine + other * sine, rest], axis=1).astype(jnp.bfloat16)

    queries = [turned(ordered[0], h) for h in range(heads)]
    new_keys = [turned(ordered[1], h) for h in range(heads)]
    new_values = ordered[2].astype(jnp.bfloat16)
    scale = HEAD_DIM ** (-0.5)
    line, at = iotas((here, prompt_len))
    tail_line, tail_at = iotas((here, samples * tail_len))
    fresh_line, fresh_at = iotas((here, here))
    fresh_keep = (fresh_at // fresh == fresh_line // fresh) & (fresh_at <= fresh_line)
    sample, _ = iotas((here, 1))
    attended = [[None] * requests for _ in range(heads)]
    for r in range(requests):
        lengths = jnp.zeros((here, 1), jnp.int32)
        for s in range(samples):
            lengths = jnp.where(sample // fresh == s, tlen_ref[r, s], lengths)
        keep = at < plen_ref[r]
        tail_keep = (tail_at // tail_len == tail_line // fresh) & (tail_at % tail_len < lengths)
        own = slice(r * here, (r + 1) * here)
        for i in range(2):
            cache_copy(r, i).wait()
        weighted = []
        for h in range(heads):
            cols = slice(h * HEAD_DIM, (h + 1) * HEAD_DIM)
            query = queries[h][own]
            def scores(keys):
                return lax.dot_general(query, keys, (((1,), (1,)), ((), ())), preferred_element_type=jnp.float32) * scale
            prompt = jnp.where(keep, scores(pk[r, :, cols]), VERY_LOW)
            tail = jnp.where(tail_keep, scores(tk[r, :, cols]), VERY_LOW)
            new = jnp.where(fresh_keep, scores(new_keys[h][own]), VERY_LOW)
            top = jnp.maximum(
                jnp.max(prompt, axis=1, keepdims=True),
                jnp.maximum(jnp.max(tail, axis=1, keepdims=True), jnp.max(new, axis=1, keepdims=True)),
            )
            weights = [jnp.exp(part - top) for part in (prompt, tail, new)]
            total = sum(jnp.sum(part, axis=1, keepdims=True) for part in weights)
            weighted.append(([part.astype(jnp.bfloat16) for part in weights], total))
        for i in range(2, 4):
            cache_copy(r, i).wait()
        for h in range(heads):
            cols = slice(h * HEAD_DIM, (h + 1) * HEAD_DIM)
            weights, total = weighted[h]
            summed = jnp.dot(weights[0], pv[r, :, cols], preferred_element_type=jnp.float32)
            summed = summed + jnp.dot(weights[1], tv[r, :, cols], preferred_element_type=jnp.float32)
            summed = summed + jnp.dot(weights[2], new_values[own, cols], preferred_element_type=jnp.float32)
            attended[h][r] = (summed / total).astype(jnp.bfloat16)
    joined = jnp.concatenate([jnp.concatenate(part, axis=0) for part in attended], axis=1)
    placed = lax.dot_general(pick, joined, (((0,), (0,)), ((), ())), preferred_element_type=jnp.float32).astype(jnp.bfloat16)
    for h in range(heads):
        wo_copy(h).wait()
    out_ref[...] = jnp.dot(placed, wo[...], preferred_element_type=jnp.float32).astype(jnp.bfloat16)


def mixer_call(plen, tlen, hid, near, far, turn, wq, pk, pv, tk, tv, wo):
    parts, width, columns = wq.shape
    requests, prompt_len, _ = pk.shape
    count = near.shape[0] + far.shape[0]
    keys = prompt_len + tk.shape[1]
    return pl.pallas_call(
        mixer_body,
        out_shape=jax.ShapeDtypeStruct((count, width), jnp.bfloat16),
        in_specs=[SMEM] * 3 + [VMEM] * 3 + [HBM] * 6,
        out_specs=VMEM,
        scratch_shapes=[pltpu.VMEM(a.shape, jnp.bfloat16) for a in (wq, pk, pv, tk, tv, wo)]
        + [
            pltpu.SemaphoreType.DMA((parts, CUT)),
            pltpu.SemaphoreType.DMA((requests, 4)),
            pltpu.SemaphoreType.DMA((columns // HEAD_DIM,)),
        ],
        compiler_params=pltpu.CompilerParams(vmem_limit_bytes=60 * MIB),
        cost_estimate=pl.CostEstimate(
            flops=2 * count * columns * (parts * width + 2 * keys + width),
            bytes_accessed=2 * columns * (parts * width + 2 * requests * keys + width),
            transcendentals=count * keys * (columns // HEAD_DIM),
        ),
        name="mixer",
    )(plen, tlen, hid, near, far, turn, wq, pk, pv, tk, tv, wo)


def mlp_body(place_ref, own_ref, other_ref, near_ref, far_ref, *refs):
    packed, (out_own, out_other), (ups, downs, up_sem, down_sem) = refs[:4], refs[4:6], refs[6:]
    blocks = ups.shape[0]
    def up_copy(p):
        return pltpu.make_async_copy(
            packed[p].at[pl.ds(0, blocks)], ups.at[:, :, pl.ds(p * LANES, LANES)], up_sem.at[p]
        )
    def down_copy(p):
        return pltpu.make_async_copy(
            packed[p].at[pl.ds(blocks, blocks)], downs.at[:, pl.ds(p * LANES, LANES), :], down_sem.at[p]
        )
    for p in range(4):
        up_copy(p).start()
    for p in range(4):
        down_copy(p).start()
    rows = jnp.concatenate([own_ref[...], other_ref[...]], axis=0)
    units = ups.shape[2]
    for p in range(4):
        up_copy(p).wait()
    hidden = jnp.dot(rows, ups[...].reshape(blocks * LANES, units), preferred_element_type=jnp.float32)
    hidden = jax.nn.gelu(hidden, approximate=True).astype(jnp.bfloat16)
    for p in range(4):
        down_copy(p).wait()
    half = own_ref.shape[0]
    for j in range(0, blocks, 2):
        result = jnp.dot(
            hidden, jnp.concatenate([downs[j], downs[j + 1]], axis=1), preferred_element_type=jnp.float32
        ).astype(jnp.bfloat16)
        cols = slice(j * LANES, (j + 2) * LANES)
        out_own[:, cols] = result[:half]
        out_other[:, cols] = result[half:]
    count = near_ref.shape[0] // 2
    for i in range(2):
        at = pl.ds(pl.multiple_of((place_ref[0] ^ i) * count, count), count)
        part = pl.ds(i * count, count)
        out_own[at] = (
            out_own[at].astype(jnp.float32)
            + near_ref[part].astype(jnp.float32)
            + far_ref[part].astype(jnp.float32)
        ).astype(jnp.bfloat16)


def mlp_call(place, own, other, near, far, packed):
    count, width = own.shape
    units = 4 * LANES
    blocks = width // LANES
    return pl.pallas_call(
        mlp_body,
        out_shape=[jax.ShapeDtypeStruct((count, width), jnp.bfloat16)] * 2,
        in_specs=[SMEM] + [VMEM] * 4 + [HBM] * 4,
        out_specs=[VMEM] * 2,
        scratch_shapes=[
            pltpu.VMEM((blocks, LANES, units), jnp.bfloat16),
            pltpu.VMEM((blocks, units, LANES), jnp.bfloat16),
            pltpu.SemaphoreType.DMA((4,)),
            pltpu.SemaphoreType.DMA((4,)),
        ],
        compiler_params=pltpu.CompilerParams(vmem_limit_bytes=24 * MIB),
        cost_estimate=pl.CostEstimate(
            flops=8 * count * width * units,
            bytes_accessed=2 * (4 * count * width + 2 * units * width),
            transcendentals=2 * count * units,
        ),
        name="mlp",
    )(place, own, other, near, far, *packed)


def add_body(a_ref, b_ref, out_ref):
    out_ref[...] = (a_ref[...].astype(jnp.float32) + b_ref[...].astype(jnp.float32)).astype(jnp.bfloat16)


def add_call(a, b):
    return pl.pallas_call(
        add_body,
        out_shape=jax.ShapeDtypeStruct(b.shape, jnp.bfloat16),
        in_specs=[VMEM] * 2,
        out_specs=VMEM,
        compiler_params=pltpu.CompilerParams(vmem_limit_bytes=8 * MIB),
        name="add",
    )(a, b)


def end_body(tokens_ref, returned_ref, gain_ref, score_ref, next_ref, out_ref, rows):
    requests, samples, fresh, width = tokens_ref.shape
    for r in range(requests):
        for s in range(samples):
            at = (r * samples + s) * fresh
            rows[at : at + fresh] = tokens_ref[r, s].astype(jnp.float32)
    added = returned_ref[0].astype(jnp.float32)
    for i in range(1, returned_ref.shape[0]):
        added = added + returned_ref[i].astype(jnp.float32)
    final = rows[...] + added
    scores = jnp.sum(
        normalised(final, gain_ref[...]) * score_ref[...].astype(jnp.float32), axis=1, keepdims=True
    )
    rows[...] = final
    row, col = iotas((final.shape[0], fresh))
    for r in range(requests):
        for s in range(samples):
            at = (r * samples + s) * fresh
            next_ref[r, s] = rows[at : at + fresh].astype(jnp.bfloat16)
            out_ref[r, s : s + 1] = jnp.sum(jnp.where(row == at + col, scores, 0.0), axis=0, keepdims=True)


def end_call(tokens, returned, gain, score_weight):
    width = tokens.shape[-1]
    return pl.pallas_call(
        end_body,
        out_shape=[
            jax.ShapeDtypeStruct(tokens.shape, jnp.bfloat16),
            jax.ShapeDtypeStruct(tokens.shape[:-1], jnp.float32),
        ],
        in_specs=[VMEM] * 4,
        out_specs=[VMEM] * 2,
        scratch_shapes=[pltpu.VMEM((returned.shape[1], width), jnp.float32)],
        compiler_params=pltpu.CompilerParams(vmem_limit_bytes=8 * MIB),
        name="end",
    )(tokens, returned, gain.reshape(1, width), score_weight.reshape(1, width))


def rotation_tables(positions):
    lane = jnp.arange(LANES, dtype=jnp.int32)
    frequency = 10000.0 ** (-((lane // 2).astype(jnp.float32) * (2.0 / ROT)))
    angles = positions.astype(jnp.float32)[:, None] * frequency
    sign = jnp.where(lane % 2 == 0, -1.0, 1.0)
    rotated = lane < ROT
    return jnp.stack(
        [jnp.where(rotated, jnp.cos(angles), 1.0), jnp.where(rotated, jnp.sin(angles) * sign, 0.0)]
    )


def shards(
    tokens,
    input_gain,
    qkv_weight,
    out_weight,
    in_weight,
    down_weight,
    final_gain,
    score_weight,
    prompt_keys,
    prompt_values,
    tail_keys,
    tail_values,
    prompt_lengths,
    tail_lengths,
):
    req_dev, samp_dev, fresh, width = tokens.shape
    own_rows = req_dev * samp_dev * fresh
    groups = token_groups()
    sharing = len(groups[0])
    normed, copies, own_weights = start_call(tokens, input_gain, in_weight, down_weight, sharing)

    near = jnp.concatenate([normed, swap(normed, "u"), swap(normed, "w"), swap(normed, "u", "w")], axis=0)
    near, late_weights = lax.optimization_barrier((near, own_weights))
    far = swap(near, "c")
    packed = [own_weights] + [from_neighbour(late_weights, axis) for axis in "xyz"]

    def exchange(values):
        return lax.all_to_all(values, AXES, 0, 0, axis_index_groups=groups, tiled=True)

    visitors = exchange(copies).reshape(sharing * own_rows, width)
    positions = (
        prompt_lengths[:, None, None]
        + tail_lengths[:, :, None]
        + jnp.arange(fresh, dtype=jnp.int32)[None, None, :]
    )
    slab = tail_keys.shape[-1]
    partial = mixer_call(
        prompt_lengths,
        tail_lengths,
        lax.axis_index(HID).astype(jnp.int32).reshape(1),
        near,
        far,
        rotation_tables(positions.reshape(-1)),
        jnp.transpose(qkv_weight, (1, 0, 2)),
        prompt_keys,
        prompt_values,
        tail_keys.reshape(req_dev, -1, slab),
        tail_values.reshape(req_dev, -1, slab),
        out_weight,
    )
    other_visitors = swap(visitors, "c")
    half = partial.shape[0] // 2
    projected = add_call(partial[:half], swap(partial[half:], "c"))
    half = projected.shape[0] // 2
    projected_far = swap(projected[half:], "w")
    projected, projected_far, packed, visitors, other_visitors = lax.optimization_barrier(
        (projected, projected_far, packed, visitors, other_visitors)
    )

    place = lax.axis_index("y") * SIDE + lax.axis_index("x") // 2 * 2 + lax.axis_index("u")
    place = place.astype(jnp.int32).reshape(1)
    mine, others = mlp_call(place, visitors, other_visitors, projected[:half], projected_far, packed)
    summed = add_call(mine, swap(others, "c"))
    returned = exchange(summed.reshape(sharing, own_rows, width))
    next_hidden, sample_scores = end_call(tokens, returned, final_gain, score_weight)
    return (next_hidden, sample_scores)


def solution(mesh):
    grid = Mesh(mesh.devices.reshape(SIDE, SIDE, 2, 2, CORES), AXES)
    placed = (
        P(REQ, HID, None, None),
        P(),
        P(None, None, HID),
        P(HID, None),
        P(None, REQ + HID),
        P(REQ + HID, None),
        P(),
        P(),
        P(REQ, None, HID),
        P(REQ, None, HID),
        P(REQ, None, None, HID),
        P(REQ, None, None, HID),
        P(REQ),
        P(REQ, None),
    )
    return jax.shard_map(
        shards,
        mesh=grid,
        in_specs=placed,
        out_specs=(P(REQ, HID, None, None), P(REQ, HID, None)),
        check_vma=False,
    )
```

time: 823 us -> 99.7 us (0.12)
  waiting for transfers between devices: 735 us -> 36.7 us
  matrix products: 38.6 us -> 0 us
  starting transfers between devices: 0.12 us -> 28.8 us
  Pallas kernels: 0 us -> 28.5 us
  local copies, waits for them, and re-layouts: 26.3 us -> 2.6 us
  between operations: 14.1 us -> 0.83 us
    reduce_scatter x2 -> x0, waiting for transfers between devices: 680 us -> none  [the longest x1 667 us: shards(): lax.psum_scatter(jnp.dot(hidden_units, down_weight, preferred_element_typ...]
    all_gather x1 -> x0, waiting for transfers between devices: 55.2 us -> none  [shards(): gathered = lax.all_gather(normed, ('req', 'hid'), axis=0, tiled=True)]
    dot_general x9 -> x0, matrix products: 38.6 us -> none  [the longest x1 14.4 us: shards(): jnp.dot(hidden_units, down_weight, preferred_element_type=jnp.float32)]
    pallas_call x0 -> x6, Pallas kernels: none -> 28.5 us  [the longest x1 16.3 us: mixer_call(): pl.pallas_call(mixer_body, out_shape=jax.ShapeDtypeStruct((count, width),...]
    all_to_all x0 -> x2, waiting for transfers between devices: none -> 21.1 us  [exchange(): lax.all_to_all(values, AXES, 0, 0, axis_index_groups=groups, tiled=True)]
    unnamed x13 -> x16, local copies, waits for them, and re-layouts: 17.6 us -> 0.75 us
    all_to_all x0 -> x2, starting transfers between devices: none -> 16.6 us  [exchange(): lax.all_to_all(values, AXES, 0, 0, axis_index_groups=groups, tiled=True)]
    ppermute x0 -> x11, waiting for transfers between devices: none -> 15.6 us  [the longest x8 13 us: swap(): return lax.ppermute(values, axes, [(i, last - i) for i in range(last + 1)])]
  transfers between devices with their start and end apart: 3 -> 13, of which waited for: 3 -> 6; matrix products, arithmetic and copies ran while one was open for 4% -> 4% of each run, Pallas kernels for 0% -> 16%
where the time goes in v2:
time: 99.7 us; the launch traced here: 99.3 us
  waiting for transfers between devices  36.7 us (37%)
  starting transfers between devices  28.8 us (29%)
  Pallas kernels  28.5 us (29%)
  local copies, waits for them, and re-layouts  2.6 us (3%)
  other arithmetic  1.88 us (2%)
    all_to_all x2, waiting for transfers between devices, exchange(): lax.all_to_all(values, AXES, 0, 0, axis_index_groups=groups, tiled=True)  21.1 us
    all_to_all x2, starting transfers between devices, exchange(): lax.all_to_all(values, AXES, 0, 0, axis_index_groups=groups, tiled=True)  16.6 us
    pallas_call x1, Pallas kernels, mixer_call(): pl.pallas_call(mixer_body, out_shape=jax.ShapeDtypeStruct((count, width),...  16.3 us
    ppermute x8, waiting for transfers between devices, swap(): return lax.ppermute(values, axes, [(i, last - i) for i in range(last + 1)])  13 us
    ppermute x8, starting transfers between devices, swap(): return lax.ppermute(values, axes, [(i, last - i) for i in range(last + 1)])  7.27 us
    pallas_call x1, Pallas kernels, mlp_call(): pl.pallas_call(mlp_body, out_shape=[jax.ShapeDtypeStruct((count, width),...  5.98 us
    ppermute x3, starting transfers between devices, from_neighbour(): return lax.ppermute(values, AXES, moves)  4.92 us
    pallas_call x1, Pallas kernels, start_call(): pl.pallas_call(start_body, out_shape=[jax.ShapeDtypeStruct((own_rows, wid...  3.79 us
  transfers between devices with their start and end apart: 13, of which 6 were waited for; matrix products, arithmetic and copies ran while one was open for 4% of the time, Pallas kernels for 16%

profile of v2, /device:TPU:0, one launch (start us, length us, event | category | flops | bytes accessed | tf_op | source)
XLA Modules:
  0.0 99.3 jit_solution(2521891908754380934)
XLA Ops:
  0.6 0.0 copy-start.6
  0.6 0.0 copy-start.7
  0.7 3.8 %start.1 = (bf16[8,4096]{1,0:T(8,128)(2,1)}, bf16[16,8,4096]{2,1,0:T(8,128)(2,1)}, bf16[64,128,128]{2,1,0:T(8,128)(2,1)}) custom-call(bf16[2,2,2,4096]{3,2,1,0:T(2,128)(2,1)} %tokens_ref.1, f32[1,4096]{1,0:T(1,128)} %bitcast.17, bf16[32,128,128]{2,1,0:T(8,128)(2,1)} %bitcast.16, bf16[128,4096]{1,0:T(8,128)(2,1)} %down_hbm.1), custom_call_target="tpu_custom_call" | custom-call | tf_op jit(solution)/shard_map/start/pallas_call | solution.py:108
  4.4 0.0 copy-start
  4.5 4.0 %collective-permute-start = (bf16[8,4096]{1,0:T(8,128)(2,1)}, bf16[8,4096]{1,0:T(8,128)(2,1)S(1)}, u32[]{:S(2)}, u32[]{:S(2)}) collective-permute-start(bf16[8,4096]{1,0:T(8,128)(2,1)} %get-tuple-element.17), channel_id=1, source_target_pairs={{0,4},{4,0},{1,5},{5,1},{2,6},{6,2},{3,7},{7,3},{8,12},{12,8},{9,1... | collective-permute-start | bytes 196616 | tf_op jit(solution)/shard_map/ppermute | solution.py:57
  8.5 1.0 %collective-permute-start.1 = (bf16[8,4096]{1,0:T(8,128)(2,1)}, bf16[8,4096]{1,0:T(8,128)(2,1)S(1)}, u32[]{:S(2)}, u32[]{:S(2)}) collective-permute-start(bf16[8,4096]{1,0:T(8,128)(2,1)} %get-tuple-element.17), channel_id=1, source_target_pairs={{0,2},{2,0},{1,3},{3,1},{4,6},{6,4},{5,7},{7,5},{8,10},{10,8},{9,1... | collective-permute-start | bytes 196616 | tf_op jit(solution)/shard_map/ppermute | solution.py:57
  9.5 0.0 collective-permute-start.2
  9.5 9.5 %all-to-all-start = ((bf16[16,8,4096]{2,1,0:T(8,128)(2,1)}), bf16[16,8,4096]{2,1,0:T(8,128)(2,1)S(1)}, u32[]{:S(2)}, u32[]{:S(2)}) async-start(bf16[16,8,4096]{2,1,0:T(8,128)(2,1)} %get-tuple-element.21), calls=%async_computation | async-start | bytes 2097152 | tf_op jit(solution)/shard_map/all_to_all | solution.py:430
  19.1 0.0 copy-done.6
  19.1 0.0 copy-done.7
  19.1 0.1 broadcast_add_fusion
  19.2 0.0 collective-permute-done
  19.2 0.0 collective-permute-done.1
  19.2 0.0 collective-permute-done.2
  19.2 0.9 pad_maximum_fusion.near_ref
  20.1 0.0 copy-start.3
  20.1 0.0 copy-done
  20.1 0.7 collective-permute-start.6
  20.8 3.2 %collective-permute-start.7 = (bf16[64,128,128]{2,1,0:T(8,128)(2,1)S(1)}, bf16[64,128,128]{2,1,0:T(8,128)(2,1)}, u32[]{:S(2)}, u32[]{:S(2)}) collective-permute-start(bf16[64,128,128]{2,1,0:T(8,128)(2,1)S(1)} %copy-done), channel_id=1, source_target_pairs={{0,32},{1,97},{2,34},{3,99},{4,36},{5,101},{6,38},{7,103},{8,40},{... | collective-permute-start | bytes 6291464 | tf_op jit(solution)/shard_map/ppermute | solution.py:52
  24.0 1.0 %collective-permute-start.8 = (bf16[64,128,128]{2,1,0:T(8,128)(2,1)S(1)}, bf16[64,128,128]{2,1,0:T(8,128)(2,1)}, u32[]{:S(2)}, u32[]{:S(2)}) collective-permute-start(bf16[64,128,128]{2,1,0:T(8,128)(2,1)S(1)} %copy-done), channel_id=1, source_target_pairs={{0,2},{1,7},{2,4},{3,1},{4,6},{5,3},{6,0},{7,5},{8,10},{9,15},{10,... | collective-permute-start | bytes 6291464 | tf_op jit(solution)/shard_map/ppermute | solution.py:52
  25.0 0.1 add_convert_fusion
  25.1 0.1 convert_element_type.18
  25.2 1.3 %collective-permute-start.3 = (bf16[32,4096]{1,0:T(8,128)(2,1)S(1)}, bf16[32,4096]{1,0:T(8,128)(2,1)S(1)}, u32[]{:S(2)}, u32[]{:S(2)}) collective-permute-start(bf16[32,4096]{1,0:T(8,128)(2,1)S(1)} %pad_maximum_fusion.near_ref), channel_id=1, source_target_pairs={{0,1},{1,0},{2,3},{3,2},{4,5},{5,4},{6,7},{7,6},{8,9},{9,8},{10,11... | collective-permute-start | bytes 786440 | tf_op jit(solution)/shard_map/ppermute | solution.py:57
  26.5 0.2 fusion
  26.7 0.6 pad_maximum_fusion.1.turn_ref
  27.4 0.3 collective-permute-done.3.far_ref
  27.7 0.0 copy-start.4
  27.7 0.0 copy-done.3
  27.7 0.7 copy-done.4
  28.4 16.3 %mixer.1 = bf16[64,4096]{1,0:T(8,128)(2,1)} custom-call(s32[2]{0:T(128)} %plen_ref.1, s32[2,16]{1,0:T(2,128)} %tlen_ref.1, s32[1]{0:T(128)} %bitcast.1.hid_ref, bf16[32,4096]{1,0:T(8,128)(2,1)} %copy-done.3, bf16[32,4096]{1,0:T(8,128)(2,1)} %copy-done.4, f32[2,64,128]{2,1,0:T(8,128)} %pad_maximum_fusion.1.turn_ref, bf16[3,4096,512]{2,1,0:T(8,128)(2,1)} %bitcast.13, ...), custom_call_target="tpu_custom_call" | custom-call | flops 1476395008 | bytes 29360128 | tf_op jit(solution)/shard_map/mixer/pallas_call | solution.py:250
  44.7 0.0 all-to-all-done
  44.7 0.5 collective-permute-start.9
  45.2 1.1 %fusion.7 = (bf16[32,4096]{1,0:T(8,128)(2,1)S(1)}, bf16[32,4096]{1,0:T(8,128)(2,1)S(1)}) fusion(bf16[64,4096]{1,0:T(8,128)(2,1)} %mixer.1), kind=kLoop, calls=%fused_computation.20 | loop fusion | bytes 1048576 | tf_op jit(solution)/shard_map/slice | solution.py:455
  46.3 0.2 collective-permute-start.4
  46.5 1.4 %collective-permute-done.4.b_ref = bf16[32,4096]{1,0:T(8,128)(2,1)S(1)} collective-permute-done((bf16[32,4096]{1,0:T(8,128)(2,1)S(1)}, bf16[32,4096]{1,0:T(8,128)(2,1)S(1)}, u32[]{:S(2)}, u32[]{:S(2)}) %collective-permute-start.4) | collective-permute-done | bytes 262176 | tf_op jit(solution)/shard_map/ppermute | solution.py:57
  47.9 0.1 add.76
  47.9 0.7 slice.18
  48.6 0.1 collective-permute-start.5
  48.7 8.7 %collective-permute-done.5.far_ref = bf16[16,4096]{1,0:T(8,128)(2,1)S(1)} collective-permute-done((bf16[16,4096]{1,0:T(8,128)(2,1)}, bf16[16,4096]{1,0:T(8,128)(2,1)S(1)}, u32[]{:S(2)}, u32[]{:S(2)}) %collective-permute-start.5) | collective-permute-done | bytes 131104 | tf_op jit(solution)/shard_map/ppermute | solution.py:57
  57.4 0.0 collective-permute-done.9.other_ref
  57.4 0.0 collective-permute-done.6.refs_1_
  57.4 0.0 collective-permute-done.7.refs_2_
  57.4 2.5 %collective-permute-done.8.refs_3_ = bf16[64,128,128]{2,1,0:T(8,128)(2,1)} collective-permute-done((bf16[64,128,128]{2,1,0:T(8,128)(2,1)S(1)}, bf16[64,128,128]{2,1,0:T(8,128)(2,1)}, u32[]{:S(2)}, u32[]{:S(2)}) %collective-permute-start.8) | collective-permute-done | bytes 2097184 | tf_op jit(solution)/shard_map/ppermute | solution.py:52
  60.0 6.0 %mlp.1 = (bf16[128,4096]{1,0:T(8,128)(2,1)S(1)}, bf16[128,4096]{1,0:T(8,128)(2,1)S(1)}) custom-call(s32[1]{0:T(128)} %bitcast.place_ref, bf16[128,4096]{1,0:T(8,128)(2,1)S(1)} %bitcast.11, bf16[128,4096]{1,0:T(8,128)(2,1)} %collective-permute-done.9.other_ref, bf16[16,4096]{1,0:T(8,128)(2,1)S(1)} %slice.15.near_ref, ...), custom_call_target="tpu_custom_call" | custom-call | flops 2147483648 | bytes 12582912 | tf_op jit(solution)/shard_map/mlp/pallas_call | solution.py:317
  65.9 0.1 collective-permute-start.10
  66.0 2.6 %collective-permute-done.10.b_ref = bf16[128,4096]{1,0:T(8,128)(2,1)S(1)} collective-permute-done((bf16[128,4096]{1,0:T(8,128)(2,1)S(1)}, bf16[128,4096]{1,0:T(8,128)(2,1)S(1)}, u32[]{:S(2)}, u32[]{:S(2)}) %collective-permute-start.10) | collective-permute-done | bytes 1048608 | tf_op jit(solution)/shard_map/ppermute | solution.py:57
  68.7 0.0 copy-start.5
  68.7 0.0 copy-start.1
  68.7 0.0 copy-start.2
  68.7 1.3 %add.77 = bf16[128,4096]{1,0:T(8,128)(2,1)} custom-call(bf16[128,4096]{1,0:T(8,128)(2,1)S(1)} %get-tuple-element.30.a_ref, bf16[128,4096]{1,0:T(8,128)(2,1)S(1)} %collective-permute-done.10.b_ref), custom_call_target="tpu_custom_call" | custom-call | tf_op jit(solution)/shard_map/add/pallas_call | solution.py:343
  69.9 7.1 %all-to-all-start.1 = ((bf16[16,8,4096]{2,1,0:T(8,128)(2,1)}), bf16[16,8,4096]{2,1,0:T(8,128)(2,1)S(1)}, u32[]{:S(2)}, u32[]{:S(2)}) async-start(bf16[16,8,4096]{2,1,0:T(8,128)(2,1)} %bitcast.8), calls=%async_computation.1 | async-start | bytes 2097152 | tf_op jit(solution)/shard_map/all_to_all | solution.py:430
  77.0 0.0 copy-done.5
  77.1 21.1 %all-to-all-done.1.returned_ref = bf16[16,8,4096]{2,1,0:T(8,128)(2,1)S(1)} async-done(((bf16[16,8,4096]{2,1,0:T(8,128)(2,1)}), bf16[16,8,4096]{2,1,0:T(8,128)(2,1)S(1)}, u32[]{:S(2)}, u32[]{:S(2)}) %all-to-all-start.1) | async-done | bytes 1048608 | tf_op jit(solution)/shard_map/all_to_all | solution.py:430
  98.2 0.0 copy-done.1
  98.2 0.0 copy-done.2
  98.2 1.1 %end.1 = (bf16[2,2,2,4096]{3,2,1,0:T(2,128)(2,1)}, f32[2,2,2]{2,1,0:T(2,128)}) custom-call(bf16[2,2,2,4096]{3,2,1,0:T(2,128)(2,1)S(1)} %copy-done.1, bf16[16,8,4096]{2,1,0:T(8,128)(2,1)S(1)} %all-to-all-done.1.returned_ref, f32[1,4096]{1,0:T(1,128)S(1)} %bitcast.12, bf16[1,4096]{1,0:T(2,128)(2,1)S(1)} %reshape.250.score_ref), custom_call_target="tpu_custom_call" | custom-call | tf_op jit(solution)/shard_map/end/pallas_call | solution.py:377
  (4 shorter events, 0.0 us)
Async XLA Ops:
  0.6 18.4 %copy-start.6 = (s32[2,16]{1,0:T(2,128)S(1)}, s32[2,16]{1,0:T(2,128)}, u32[]{:S(2)}) copy-start(s32[2,16]{1,0:T(2,128)} %tlen_ref.1) | copy-start | bytes 388
  0.6 18.4 %copy-start.7 = (s32[2]{0:T(128)S(1)}, s32[2]{0:T(128)}, u32[]{:S(2)}) copy-start(s32[2]{0:T(128)} %plen_ref.1) | copy-start | bytes 28
  4.4 15.6 %copy-start = (bf16[64,128,128]{2,1,0:T(8,128)(2,1)S(1)}, bf16[64,128,128]{2,1,0:T(8,128)(2,1)}, u32[]{:S(2)}) copy-start(bf16[64,128,128]{2,1,0:T(8,128)(2,1)} %get-tuple-element.26.refs_0_) | copy-start | bytes 6291460
  4.5 14.7 %collective-permute-start = (bf16[8,4096]{1,0:T(8,128)(2,1)}, bf16[8,4096]{1,0:T(8,128)(2,1)S(1)}, u32[]{:S(2)}, u32[]{:S(2)}) collective-permute-start(bf16[8,4096]{1,0:T(8,128)(2,1)} %get-tuple-element.17), channel_id=1, source_target_pairs={{0,4},{4,0},{1,5},{5,1},{2,6},{6,2},{3,7},{7,3},{8,12},{12,8},{9,1... | collective-permute-start | bytes 196616 | tf_op jit(solution)/shard_map/ppermute | solution.py:57
  8.5 10.7 %collective-permute-start.1 = (bf16[8,4096]{1,0:T(8,128)(2,1)}, bf16[8,4096]{1,0:T(8,128)(2,1)S(1)}, u32[]{:S(2)}, u32[]{:S(2)}) collective-permute-start(bf16[8,4096]{1,0:T(8,128)(2,1)} %get-tuple-element.17), channel_id=1, source_target_pairs={{0,2},{2,0},{1,3},{3,1},{4,6},{6,4},{5,7},{7,5},{8,10},{10,8},{9,1... | collective-permute-start | bytes 196616 | tf_op jit(solution)/shard_map/ppermute | solution.py:57
  9.5 9.7 %collective-permute-start.2 = (bf16[8,4096]{1,0:T(8,128)(2,1)}, bf16[8,4096]{1,0:T(8,128)(2,1)}, u32[]{:S(2)}, u32[]{:S(2)}) collective-permute-start(bf16[8,4096]{1,0:T(8,128)(2,1)} %get-tuple-element.17), channel_id=1, source_target_pairs={{0,6},{2,4},{4,2},{6,0},{1,7},{3,5},{5,3},{7,1},{8,14},{10,12},{12... | collective-permute-start | bytes 196616 | tf_op jit(solution)/shard_map/ppermute | solution.py:57
  9.5 35.2 %all-to-all-start = ((bf16[16,8,4096]{2,1,0:T(8,128)(2,1)}), bf16[16,8,4096]{2,1,0:T(8,128)(2,1)S(1)}, u32[]{:S(2)}, u32[]{:S(2)}) async-start(bf16[16,8,4096]{2,1,0:T(8,128)(2,1)} %get-tuple-element.21), calls=%async_computation | async-start | bytes 2097152 | tf_op jit(solution)/shard_map/all_to_all | solution.py:430
  20.1 7.6 %copy-start.3 = (bf16[32,4096]{1,0:T(8,128)(2,1)}, bf16[32,4096]{1,0:T(8,128)(2,1)S(1)}, u32[]{:S(2)}) copy-start(bf16[32,4096]{1,0:T(8,128)(2,1)S(1)} %pad_maximum_fusion.near_ref) | copy-start | bytes 786436
  20.1 37.3 %collective-permute-start.6 = (bf16[64,128,128]{2,1,0:T(8,128)(2,1)S(1)}, bf16[64,128,128]{2,1,0:T(8,128)(2,1)}, u32[]{:S(2)}, u32[]{:S(2)}) collective-permute-start(bf16[64,128,128]{2,1,0:T(8,128)(2,1)S(1)} %copy-done), channel_id=1, source_target_pairs={{0,8},{1,25},{2,10},{3,27},{4,12},{5,29},{6,14},{7,31},{8,16},{9,1... | collective-permute-start | bytes 6291464 | tf_op jit(solution)/shard_map/ppermute | solution.py:52
  20.8 36.7 %collective-permute-start.7 = (bf16[64,128,128]{2,1,0:T(8,128)(2,1)S(1)}, bf16[64,128,128]{2,1,0:T(8,128)(2,1)}, u32[]{:S(2)}, u32[]{:S(2)}) collective-permute-start(bf16[64,128,128]{2,1,0:T(8,128)(2,1)S(1)} %copy-done), channel_id=1, source_target_pairs={{0,32},{1,97},{2,34},{3,99},{4,36},{5,101},{6,38},{7,103},{8,40},{... | collective-permute-start | bytes 6291464 | tf_op jit(solution)/shard_map/ppermute | solution.py:52
  24.0 35.9 %collective-permute-start.8 = (bf16[64,128,128]{2,1,0:T(8,128)(2,1)S(1)}, bf16[64,128,128]{2,1,0:T(8,128)(2,1)}, u32[]{:S(2)}, u32[]{:S(2)}) collective-permute-start(bf16[64,128,128]{2,1,0:T(8,128)(2,1)S(1)} %copy-done), channel_id=1, source_target_pairs={{0,2},{1,7},{2,4},{3,1},{4,6},{5,3},{6,0},{7,5},{8,10},{9,15},{10,... | collective-permute-start | bytes 6291464 | tf_op jit(solution)/shard_map/ppermute | solution.py:52
  25.2 2.5 %collective-permute-start.3 = (bf16[32,4096]{1,0:T(8,128)(2,1)S(1)}, bf16[32,4096]{1,0:T(8,128)(2,1)S(1)}, u32[]{:S(2)}, u32[]{:S(2)}) collective-permute-start(bf16[32,4096]{1,0:T(8,128)(2,1)S(1)} %pad_maximum_fusion.near_ref), channel_id=1, source_target_pairs={{0,1},{1,0},{2,3},{3,2},{4,5},{5,4},{6,7},{7,6},{8,9},{9,8},{10,11... | collective-permute-start | bytes 786440 | tf_op jit(solution)/shard_map/ppermute | solution.py:57
  27.7 0.7 copy-start.4
  44.7 12.7 %collective-permute-start.9 = (bf16[128,4096]{1,0:T(8,128)(2,1)S(1)}, bf16[128,4096]{1,0:T(8,128)(2,1)}, u32[]{:S(2)}, u32[]{:S(2)}) collective-permute-start(bf16[128,4096]{1,0:T(8,128)(2,1)S(1)} %bitcast.10), channel_id=1, source_target_pairs={{0,1},{1,0},{2,3},{3,2},{4,5},{5,4},{6,7},{7,6},{8,9},{9,8},{10,11... | collective-permute-start | bytes 3145736 | tf_op jit(solution)/shard_map/ppermute | solution.py:57
  46.3 1.6 %collective-permute-start.4 = (bf16[32,4096]{1,0:T(8,128)(2,1)S(1)}, bf16[32,4096]{1,0:T(8,128)(2,1)S(1)}, u32[]{:S(2)}, u32[]{:S(2)}) collective-permute-start(bf16[32,4096]{1,0:T(8,128)(2,1)S(1)} %get-tuple-element.32), channel_id=1, source_target_pairs={{0,1},{1,0},{2,3},{3,2},{4,5},{5,4},{6,7},{7,6},{8,9},{9,8},{10,11... | collective-permute-start | bytes 786440 | tf_op jit(solution)/shard_map/ppermute | solution.py:57
  48.6 8.8 %collective-permute-start.5 = (bf16[16,4096]{1,0:T(8,128)(2,1)}, bf16[16,4096]{1,0:T(8,128)(2,1)S(1)}, u32[]{:S(2)}, u32[]{:S(2)}) collective-permute-start(bf16[16,4096]{1,0:T(8,128)(2,1)} %slice.18), channel_id=1, source_target_pairs={{0,2},{2,0},{1,3},{3,1},{4,6},{6,4},{5,7},{7,5},{8,10},{10,8},{9,1... | collective-permute-start | bytes 393224 | tf_op jit(solution)/shard_map/ppermute | solution.py:57
  65.9 2.7 %collective-permute-start.10 = (bf16[128,4096]{1,0:T(8,128)(2,1)S(1)}, bf16[128,4096]{1,0:T(8,128)(2,1)S(1)}, u32[]{:S(2)}, u32[]{:S(2)}) collective-permute-start(bf16[128,4096]{1,0:T(8,128)(2,1)S(1)} %get-tuple-element.31), channel_id=1, source_target_pairs={{0,1},{1,0},{2,3},{3,2},{4,5},{5,4},{6,7},{7,6},{8,9},{9,8},{10,11... | collective-permute-start | bytes 3145736 | tf_op jit(solution)/shard_map/ppermute | solution.py:57
  68.7 8.4 %copy-start.5 = (bf16[4096]{0:T(1024)(128)(2,1)S(1)}, bf16[4096]{0:T(1024)(128)(2,1)}, u32[]{:S(2)}) copy-start(bf16[4096]{0:T(1024)(128)(2,1)} %param.21) | copy-start | bytes 24580
  68.7 29.5 %copy-start.1 = (bf16[2,2,2,4096]{3,2,1,0:T(2,128)(2,1)S(1)}, bf16[2,2,2,4096]{3,2,1,0:T(2,128)(2,1)}, u32[]{:S(2)}) copy-start(bf16[2,2,2,4096]{3,2,1,0:T(2,128)(2,1)} %tokens_ref.1) | copy-start | bytes 196612
  68.7 29.5 %copy-start.2 = (f32[4096]{0:T(1024)S(1)}, f32[4096]{0:T(1024)}, u32[]{:S(2)}) copy-start(f32[4096]{0:T(1024)} %param.20) | copy-start | bytes 49156
  69.9 28.2 %all-to-all-start.1 = ((bf16[16,8,4096]{2,1,0:T(8,128)(2,1)}), bf16[16,8,4096]{2,1,0:T(8,128)(2,1)S(1)}, u32[]{:S(2)}, u32[]{:S(2)}) async-start(bf16[16,8,4096]{2,1,0:T(8,128)(2,1)} %bitcast.8), calls=%async_computation.1 | async-start | bytes 2097152 | tf_op jit(solution)/shard_map/all_to_all | solution.py:430

commit v3 on v2

--- a/solution.py
+++ b/solution.py
@@ -64,40 +64,42 @@
 
 
 def start_body(
-    tokens_hbm, gain_hbm, up_hbm, down_hbm, normed_ref, copies_ref, packed_hbm, tokens_ref, gain_ref, rows, packed, down_ref, sem, out_sem
+    tokens_hbm, gain_hbm, up_hbm, down_hbm, normed_ref, copies_hbm, packed_hbm, tokens_ref, gain_ref, rows, packed, down_ref, sem, out_sem, copy_sem
 ):
     requests, samples, fresh, width = tokens_ref.shape
     blocks = up_hbm.shape[0]
     upper, lower = pl.ds(0, blocks), pl.ds(blocks, blocks)
     inward = [
-        pltpu.make_async_copy(down_hbm, down_ref, sem.at[0]),
-        pltpu.make_async_copy(up_hbm, packed.at[upper], sem.at[1]),
-        pltpu.make_async_copy(tokens_hbm, tokens_ref, sem.at[2]),
-        pltpu.make_async_copy(gain_hbm, gain_ref, sem.at[3]),
+        pltpu.make_async_copy(tokens_hbm, tokens_ref, sem.at[0]),
+        pltpu.make_async_copy(gain_hbm, gain_ref, sem.at[1]),
+        pltpu.make_async_copy(down_hbm, down_ref, sem.at[2]),
+        pltpu.make_async_copy(up_hbm, packed.at[upper], sem.at[3]),
     ]
     outward = [
         pltpu.make_async_copy(packed.at[lower], packed_hbm.at[lower], out_sem.at[0]),
         pltpu.make_async_copy(packed.at[upper], packed_hbm.at[upper], out_sem.at[1]),
     ]
+    copies = [
+        pltpu.make_async_copy(normed_ref, copies_hbm.at[i], copy_sem.at[i]) for i in range(copies_hbm.shape[0])
+    ]
     for copy in inward:
         copy.start()
     inward[0].wait()
-    for j in range(blocks):
-        packed[blocks + j] = down_ref[:, j * LANES : (j + 1) * LANES]
-    outward[0].start()
     inward[1].wait()
-    outward[1].start()
-    inward[2].wait()
-    inward[3].wait()
     for r in range(requests):
         for s in range(samples):
             at = (r * samples + s) * fresh
             rows[at : at + fresh] = tokens_ref[r, s].astype(jnp.float32)
-    normed = normalised(rows[...], gain_ref[...]).astype(jnp.bfloat16)
-    normed_ref[...] = normed
-    for i in range(copies_ref.shape[0]):
-        copies_ref[i] = normed
-    for copy in outward:
+    normed_ref[...] = normalised(rows[...], gain_ref[...]).astype(jnp.bfloat16)
+    for copy in copies:
+        copy.start()
+    inward[2].wait()
+    for j in range(blocks):
+        packed[blocks + j] = down_ref[:, j * LANES : (j + 1) * LANES]
+    outward[0].start()
+    inward[3].wait()
+    outward[1].start()
+    for copy in outward + copies:
         copy.wait()
 
 
@@ -113,7 +115,7 @@
             jax.ShapeDtypeStruct((2 * blocks, LANES, LANES), jnp.bfloat16),
         ],
         in_specs=[HBM] * 4,
-        out_specs=[VMEM, VMEM, HBM],
+        out_specs=[VMEM, HBM, HBM],
         scratch_shapes=[
             pltpu.VMEM(tokens.shape, jnp.bfloat16),
             pltpu.VMEM((1, width), jnp.float32),
@@ -122,6 +124,7 @@
             pltpu.VMEM(down.shape, jnp.bfloat16),
             pltpu.SemaphoreType.DMA((4,)),
             pltpu.SemaphoreType.DMA((2,)),
+            pltpu.SemaphoreType.DMA((sharing,)),
         ],
         compiler_params=pltpu.CompilerParams(vmem_limit_bytes=60 * MIB),
         name="start",
@@ -268,8 +271,14 @@
     )(plen, tlen, hid, near, far, turn, wq, pk, pv, tk, tv, wo)
 
 
-def mlp_body(place_ref, own_ref, other_ref, near_ref, far_ref, *refs):
-    packed, (out_own, out_other), (ups, downs, up_sem, down_sem) = refs[:4], refs[4:6], refs[6:]
+def mlp_body(place_ref, own_ref, other_hbm, near_hbm, far_hbm, *refs):
+    packed, (out_own, out_other) = refs[:4], refs[4:6]
+    other_ref, near_ref, far_ref, ups, downs, row_sem, up_sem, down_sem = refs[6:]
+    row_copies = [
+        pltpu.make_async_copy(source, target, row_sem.at[i])
+        for i, (source, target) in enumerate(((other_hbm, other_ref), (near_hbm, near_ref), (far_hbm, far_ref)))
+    ]
+    row_copies[0].start()
     blocks = ups.shape[0]
     def up_copy(p):
         return pltpu.make_async_copy(
@@ -283,6 +292,9 @@
         up_copy(p).start()
     for p in range(4):
         down_copy(p).start()
+    row_copies[1].start()
+    row_copies[2].start()
+    row_copies[0].wait()
     rows = jnp.concatenate([own_ref[...], other_ref[...]], axis=0)
     units = ups.shape[2]
     for p in range(4):
@@ -299,6 +311,8 @@
         cols = slice(j * LANES, (j + 2) * LANES)
         out_own[:, cols] = result[:half]
         out_other[:, cols] = result[half:]
+    row_copies[1].wait()
+    row_copies[2].wait()
     count = near_ref.shape[0] // 2
     for i in range(2):
         at = pl.ds(pl.multiple_of((place_ref[0] ^ i) * count, count), count)
@@ -317,11 +331,15 @@
     return pl.pallas_call(
         mlp_body,
         out_shape=[jax.ShapeDtypeStruct((count, width), jnp.bfloat16)] * 2,
-        in_specs=[SMEM] + [VMEM] * 4 + [HBM] * 4,
+        in_specs=[SMEM, VMEM] + [HBM] * 7,
         out_specs=[VMEM] * 2,
         scratch_shapes=[
+            pltpu.VMEM(other.shape, jnp.bfloat16),
+            pltpu.VMEM(near.shape, jnp.bfloat16),
+            pltpu.VMEM(far.shape, jnp.bfloat16),
             pltpu.VMEM((blocks, LANES, units), jnp.bfloat16),
             pltpu.VMEM((blocks, units, LANES), jnp.bfloat16),
+            pltpu.SemaphoreType.DMA((3,)),
             pltpu.SemaphoreType.DMA((4,)),
             pltpu.SemaphoreType.DMA((4,)),
         ],

time: 99.7 us -> 98.6 us (0.989)
  Pallas kernels: 28.5 us -> 27.4 us
  transfers between devices with their start and end apart: 13 -> 13, of which waited for: 6 -> 6; matrix products, arithmetic and copies ran while one was open for 4% -> 4% of each run, Pallas kernels for 16% -> 17%
where the time goes in v3:
time: 98.6 us; the launch traced here: 98.2 us
  waiting for transfers between devices  36.6 us (37%)
  starting transfers between devices  28.8 us (29%)
  Pallas kernels  27.4 us (28%)
  local copies, waits for them, and re-layouts  2.6 us (3%)
  other arithmetic  1.88 us (2%)
    all_to_all x2, waiting for transfers between devices, exchange(): lax.all_to_all(values, AXES, 0, 0, axis_index_groups=groups, tiled=True)  21.1 us
    all_to_all x2, starting transfers between devices, exchange(): lax.all_to_all(values, AXES, 0, 0, axis_index_groups=groups, tiled=True)  16.6 us
    pallas_call x1, Pallas kernels, mixer_call(): pl.pallas_call(mixer_body, out_shape=jax.ShapeDtypeStruct((count, width),...  16.3 us
    ppermute x8, waiting for transfers between devices, swap(): return lax.ppermute(values, axes, [(i, last - i) for i in range(last + 1)])  13 us
    ppermute x8, starting transfers between devices, swap(): return lax.ppermute(values, axes, [(i, last - i) for i in range(last + 1)])  7.27 us
    pallas_call x1, Pallas kernels, mlp_call(): pl.pallas_call(mlp_body, out_shape=[jax.ShapeDtypeStruct((count, width),...  5 us
    ppermute x3, starting transfers between devices, from_neighbour(): return lax.ppermute(values, AXES, moves)  4.92 us
    pallas_call x1, Pallas kernels, start_call(): pl.pallas_call(start_body, out_shape=[jax.ShapeDtypeStruct((own_rows, wid...  3.65 us
  transfers between devices with their start and end apart: 13, of which 6 were waited for; matrix products, arithmetic and copies ran while one was open for 4% of the time, Pallas kernels for 17%

profile of v3, /device:TPU:0, one launch (start us, length us, event | category | flops | bytes accessed | tf_op | source)
XLA Modules:
  0.0 98.2 jit_solution(11107985441068034850)
XLA Ops:
  0.6 0.0 copy-start.6
  0.6 0.0 copy-start.7
  0.7 3.7 %start.1 = (bf16[8,4096]{1,0:T(8,128)(2,1)}, bf16[16,8,4096]{2,1,0:T(8,128)(2,1)}, bf16[64,128,128]{2,1,0:T(8,128)(2,1)}) custom-call(bf16[2,2,2,4096]{3,2,1,0:T(2,128)(2,1)} %tokens_ref.1, f32[1,4096]{1,0:T(1,128)} %bitcast.17, bf16[32,128,128]{2,1,0:T(8,128)(2,1)} %bitcast.16, bf16[128,4096]{1,0:T(8,128)(2,1)} %down_hbm.1), custom_call_target="tpu_custom_call" | custom-call | tf_op jit(solution)/shard_map/start/pallas_call | solution.py:110
  4.3 0.0 copy-start
  4.3 4.0 %collective-permute-start = (bf16[8,4096]{1,0:T(8,128)(2,1)}, bf16[8,4096]{1,0:T(8,128)(2,1)S(1)}, u32[]{:S(2)}, u32[]{:S(2)}) collective-permute-start(bf16[8,4096]{1,0:T(8,128)(2,1)} %get-tuple-element.17), channel_id=1, source_target_pairs={{0,4},{4,0},{1,5},{5,1},{2,6},{6,2},{3,7},{7,3},{8,12},{12,8},{9,1... | collective-permute-start | bytes 196616 | tf_op jit(solution)/shard_map/ppermute | solution.py:57
  8.4 1.0 %collective-permute-start.1 = (bf16[8,4096]{1,0:T(8,128)(2,1)}, bf16[8,4096]{1,0:T(8,128)(2,1)S(1)}, u32[]{:S(2)}, u32[]{:S(2)}) collective-permute-start(bf16[8,4096]{1,0:T(8,128)(2,1)} %get-tuple-element.17), channel_id=1, source_target_pairs={{0,2},{2,0},{1,3},{3,1},{4,6},{6,4},{5,7},{7,5},{8,10},{10,8},{9,1... | collective-permute-start | bytes 196616 | tf_op jit(solution)/shard_map/ppermute | solution.py:57
  9.4 0.0 collective-permute-start.2
  9.4 9.5 %all-to-all-start = ((bf16[16,8,4096]{2,1,0:T(8,128)(2,1)}), bf16[16,8,4096]{2,1,0:T(8,128)(2,1)S(1)}, u32[]{:S(2)}, u32[]{:S(2)}) async-start(bf16[16,8,4096]{2,1,0:T(8,128)(2,1)} %get-tuple-element.21), calls=%async_computation | async-start | bytes 2097152 | tf_op jit(solution)/shard_map/all_to_all | solution.py:448
  18.9 0.0 copy-done.6
  18.9 0.0 copy-done.7
  19.0 0.1 broadcast_add_fusion
  19.0 0.0 collective-permute-done
  19.0 0.0 collective-permute-done.1
  19.0 0.0 collective-permute-done.2
  19.0 0.9 pad_maximum_fusion.near_ref
  19.9 0.0 copy-start.3
  19.9 0.0 copy-done
  20.0 0.7 collective-permute-start.6
  20.6 3.2 %collective-permute-start.7 = (bf16[64,128,128]{2,1,0:T(8,128)(2,1)S(1)}, bf16[64,128,128]{2,1,0:T(8,128)(2,1)}, u32[]{:S(2)}, u32[]{:S(2)}) collective-permute-start(bf16[64,128,128]{2,1,0:T(8,128)(2,1)S(1)} %copy-done), channel_id=1, source_target_pairs={{0,32},{1,97},{2,34},{3,99},{4,36},{5,101},{6,38},{7,103},{8,40},{... | collective-permute-start | bytes 6291464 | tf_op jit(solution)/shard_map/ppermute | solution.py:52
  23.9 1.0 %collective-permute-start.8 = (bf16[64,128,128]{2,1,0:T(8,128)(2,1)S(1)}, bf16[64,128,128]{2,1,0:T(8,128)(2,1)}, u32[]{:S(2)}, u32[]{:S(2)}) collective-permute-start(bf16[64,128,128]{2,1,0:T(8,128)(2,1)S(1)} %copy-done), channel_id=1, source_target_pairs={{0,2},{1,7},{2,4},{3,1},{4,6},{5,3},{6,0},{7,5},{8,10},{9,15},{10,... | collective-permute-start | bytes 6291464 | tf_op jit(solution)/shard_map/ppermute | solution.py:52
  24.9 0.1 add_convert_fusion
  24.9 0.1 convert_element_type.18
  25.1 1.3 %collective-permute-start.3 = (bf16[32,4096]{1,0:T(8,128)(2,1)S(1)}, bf16[32,4096]{1,0:T(8,128)(2,1)S(1)}, u32[]{:S(2)}, u32[]{:S(2)}) collective-permute-start(bf16[32,4096]{1,0:T(8,128)(2,1)S(1)} %pad_maximum_fusion.near_ref), channel_id=1, source_target_pairs={{0,1},{1,0},{2,3},{3,2},{4,5},{5,4},{6,7},{7,6},{8,9},{9,8},{10,11... | collective-permute-start | bytes 786440 | tf_op jit(solution)/shard_map/ppermute | solution.py:57
  26.4 0.2 fusion
  26.6 0.6 pad_maximum_fusion.1.turn_ref
  27.2 0.3 collective-permute-done.3.far_ref
  27.6 0.0 copy-start.4
  27.6 0.0 copy-done.3
  27.6 0.7 copy-done.4
  28.3 16.3 %mixer.1 = bf16[64,4096]{1,0:T(8,128)(2,1)} custom-call(s32[2]{0:T(128)} %plen_ref.1, s32[2,16]{1,0:T(2,128)} %tlen_ref.1, s32[1]{0:T(128)} %bitcast.1.hid_ref, bf16[32,4096]{1,0:T(8,128)(2,1)} %copy-done.3, bf16[32,4096]{1,0:T(8,128)(2,1)} %copy-done.4, f32[2,64,128]{2,1,0:T(8,128)} %pad_maximum_fusion.1.turn_ref, bf16[3,4096,512]{2,1,0:T(8,128)(2,1)} %bitcast.13, ...), custom_call_target="tpu_custom_call" | custom-call | flops 1476395008 | bytes 29360128 | tf_op jit(solution)/shard_map/mixer/pallas_call | solution.py:253
  44.6 0.0 all-to-all-done
  44.6 0.5 collective-permute-start.9
  45.1 1.1 %fusion.7 = (bf16[32,4096]{1,0:T(8,128)(2,1)S(1)}, bf16[32,4096]{1,0:T(8,128)(2,1)S(1)}) fusion(bf16[64,4096]{1,0:T(8,128)(2,1)} %mixer.1), kind=kLoop, calls=%fused_computation.20 | loop fusion | bytes 1048576 | tf_op jit(solution)/shard_map/slice | solution.py:473
  46.1 0.2 collective-permute-start.4
  46.3 1.4 %collective-permute-done.4.b_ref = bf16[32,4096]{1,0:T(8,128)(2,1)S(1)} collective-permute-done((bf16[32,4096]{1,0:T(8,128)(2,1)S(1)}, bf16[32,4096]{1,0:T(8,128)(2,1)S(1)}, u32[]{:S(2)}, u32[]{:S(2)}) %collective-permute-start.4) | collective-permute-done | bytes 262176 | tf_op jit(solution)/shard_map/ppermute | solution.py:57
  47.7 0.1 add.76
  47.8 0.7 slice.18
  48.5 0.1 collective-permute-start.5
  48.6 8.7 %collective-permute-done.5.far_hbm = bf16[16,4096]{1,0:T(8,128)(2,1)S(1)} collective-permute-done((bf16[16,4096]{1,0:T(8,128)(2,1)}, bf16[16,4096]{1,0:T(8,128)(2,1)S(1)}, u32[]{:S(2)}, u32[]{:S(2)}) %collective-permute-start.5) | collective-permute-done | bytes 131104 | tf_op jit(solution)/shard_map/ppermute | solution.py:57
  57.3 0.0 collective-permute-done.9.other_hbm
  57.3 0.0 collective-permute-done.6.refs_1_
  57.3 0.0 collective-permute-done.7.refs_2_
  57.3 2.5 %collective-permute-done.8.refs_3_ = bf16[64,128,128]{2,1,0:T(8,128)(2,1)} collective-permute-done((bf16[64,128,128]{2,1,0:T(8,128)(2,1)S(1)}, bf16[64,128,128]{2,1,0:T(8,128)(2,1)}, u32[]{:S(2)}, u32[]{:S(2)}) %collective-permute-start.8) | collective-permute-done | bytes 2097184 | tf_op jit(solution)/shard_map/ppermute | solution.py:52
  59.8 5.0 %mlp.1 = (bf16[128,4096]{1,0:T(8,128)(2,1)S(1)}, bf16[128,4096]{1,0:T(8,128)(2,1)S(1)}) custom-call(s32[1]{0:T(128)} %bitcast.place_ref, bf16[128,4096]{1,0:T(8,128)(2,1)S(1)} %bitcast.11, bf16[128,4096]{1,0:T(8,128)(2,1)} %collective-permute-done.9.other_hbm, bf16[16,4096]{1,0:T(8,128)(2,1)S(1)} %slice.15.near_hbm, ...), custom_call_target="tpu_custom_call" | custom-call | flops 2147483648 | bytes 12582912 | tf_op jit(solution)/shard_map/mlp/pallas_call | solution.py:331
  64.8 0.1 collective-permute-start.10
  64.9 2.6 %collective-permute-done.10.b_ref = bf16[128,4096]{1,0:T(8,128)(2,1)S(1)} collective-permute-done((bf16[128,4096]{1,0:T(8,128)(2,1)S(1)}, bf16[128,4096]{1,0:T(8,128)(2,1)S(1)}, u32[]{:S(2)}, u32[]{:S(2)}) %collective-permute-start.10) | collective-permute-done | bytes 1048608 | tf_op jit(solution)/shard_map/ppermute | solution.py:57
  67.6 0.0 copy-start.5
  67.6 0.0 copy-start.1
  67.6 0.0 copy-start.2
  67.6 1.3 %add.77 = bf16[128,4096]{1,0:T(8,128)(2,1)} custom-call(bf16[128,4096]{1,0:T(8,128)(2,1)S(1)} %get-tuple-element.30.a_ref, bf16[128,4096]{1,0:T(8,128)(2,1)S(1)} %collective-permute-done.10.b_ref), custom_call_target="tpu_custom_call" | custom-call | tf_op jit(solution)/shard_map/add/pallas_call | solution.py:361
  68.8 7.1 %all-to-all-start.1 = ((bf16[16,8,4096]{2,1,0:T(8,128)(2,1)}), bf16[16,8,4096]{2,1,0:T(8,128)(2,1)S(1)}, u32[]{:S(2)}, u32[]{:S(2)}) async-start(bf16[16,8,4096]{2,1,0:T(8,128)(2,1)} %bitcast.8), calls=%async_computation.1 | async-start | bytes 2097152 | tf_op jit(solution)/shard_map/all_to_all | solution.py:448
  75.9 0.0 copy-done.5
  76.0 21.1 %all-to-all-done.1.returned_ref = bf16[16,8,4096]{2,1,0:T(8,128)(2,1)S(1)} async-done(((bf16[16,8,4096]{2,1,0:T(8,128)(2,1)}), bf16[16,8,4096]{2,1,0:T(8,128)(2,1)S(1)}, u32[]{:S(2)}, u32[]{:S(2)}) %all-to-all-start.1) | async-done | bytes 1048608 | tf_op jit(solution)/shard_map/all_to_all | solution.py:448
  97.0 0.0 copy-done.1
  97.0 0.0 copy-done.2
  97.0 1.1 %end.1 = (bf16[2,2,2,4096]{3,2,1,0:T(2,128)(2,1)}, f32[2,2,2]{2,1,0:T(2,128)}) custom-call(bf16[2,2,2,4096]{3,2,1,0:T(2,128)(2,1)S(1)} %copy-done.1, bf16[16,8,4096]{2,1,0:T(8,128)(2,1)S(1)} %all-to-all-done.1.returned_ref, f32[1,4096]{1,0:T(1,128)S(1)} %bitcast.12, bf16[1,4096]{1,0:T(2,128)(2,1)S(1)} %reshape.250.score_ref), custom_call_target="tpu_custom_call" | custom-call | tf_op jit(solution)/shard_map/end/pallas_call | solution.py:395
  (4 shorter events, 0.0 us)
Async XLA Ops:
  0.6 18.3 %copy-start.6 = (s32[2,16]{1,0:T(2,128)S(1)}, s32[2,16]{1,0:T(2,128)}, u32[]{:S(2)}) copy-start(s32[2,16]{1,0:T(2,128)} %tlen_ref.1) | copy-start | bytes 388
  0.6 18.3 %copy-start.7 = (s32[2]{0:T(128)S(1)}, s32[2]{0:T(128)}, u32[]{:S(2)}) copy-start(s32[2]{0:T(128)} %plen_ref.1) | copy-start | bytes 28
  4.3 15.6 %copy-start = (bf16[64,128,128]{2,1,0:T(8,128)(2,1)S(1)}, bf16[64,128,128]{2,1,0:T(8,128)(2,1)}, u32[]{:S(2)}) copy-start(bf16[64,128,128]{2,1,0:T(8,128)(2,1)} %get-tuple-element.26.refs_0_) | copy-start | bytes 6291460
  4.3 14.7 %collective-permute-start = (bf16[8,4096]{1,0:T(8,128)(2,1)}, bf16[8,4096]{1,0:T(8,128)(2,1)S(1)}, u32[]{:S(2)}, u32[]{:S(2)}) collective-permute-start(bf16[8,4096]{1,0:T(8,128)(2,1)} %get-tuple-element.17), channel_id=1, source_target_pairs={{0,4},{4,0},{1,5},{5,1},{2,6},{6,2},{3,7},{7,3},{8,12},{12,8},{9,1... | collective-permute-start | bytes 196616 | tf_op jit(solution)/shard_map/ppermute | solution.py:57
  8.4 10.7 %collective-permute-start.1 = (bf16[8,4096]{1,0:T(8,128)(2,1)}, bf16[8,4096]{1,0:T(8,128)(2,1)S(1)}, u32[]{:S(2)}, u32[]{:S(2)}) collective-permute-start(bf16[8,4096]{1,0:T(8,128)(2,1)} %get-tuple-element.17), channel_id=1, source_target_pairs={{0,2},{2,0},{1,3},{3,1},{4,6},{6,4},{5,7},{7,5},{8,10},{10,8},{9,1... | collective-permute-start | bytes 196616 | tf_op jit(solution)/shard_map/ppermute | solution.py:57
  9.4 9.7 %collective-permute-start.2 = (bf16[8,4096]{1,0:T(8,128)(2,1)}, bf16[8,4096]{1,0:T(8,128)(2,1)}, u32[]{:S(2)}, u32[]{:S(2)}) collective-permute-start(bf16[8,4096]{1,0:T(8,128)(2,1)} %get-tuple-element.17), channel_id=1, source_target_pairs={{0,6},{2,4},{4,2},{6,0},{1,7},{3,5},{5,3},{7,1},{8,14},{10,12},{12... | collective-permute-start | bytes 196616 | tf_op jit(solution)/shard_map/ppermute | solution.py:57
  9.4 35.2 %all-to-all-start = ((bf16[16,8,4096]{2,1,0:T(8,128)(2,1)}), bf16[16,8,4096]{2,1,0:T(8,128)(2,1)S(1)}, u32[]{:S(2)}, u32[]{:S(2)}) async-start(bf16[16,8,4096]{2,1,0:T(8,128)(2,1)} %get-tuple-element.21), calls=%async_computation | async-start | bytes 2097152 | tf_op jit(solution)/shard_map/all_to_all | solution.py:448
  19.9 7.6 %copy-start.3 = (bf16[32,4096]{1,0:T(8,128)(2,1)}, bf16[32,4096]{1,0:T(8,128)(2,1)S(1)}, u32[]{:S(2)}) copy-start(bf16[32,4096]{1,0:T(8,128)(2,1)S(1)} %pad_maximum_fusion.near_ref) | copy-start | bytes 786436
  20.0 37.3 %collective-permute-start.6 = (bf16[64,128,128]{2,1,0:T(8,128)(2,1)S(1)}, bf16[64,128,128]{2,1,0:T(8,128)(2,1)}, u32[]{:S(2)}, u32[]{:S(2)}) collective-permute-start(bf16[64,128,128]{2,1,0:T(8,128)(2,1)S(1)} %copy-done), channel_id=1, source_target_pairs={{0,8},{1,25},{2,10},{3,27},{4,12},{5,29},{6,14},{7,31},{8,16},{9,1... | collective-permute-start | bytes 6291464 | tf_op jit(solution)/shard_map/ppermute | solution.py:52
  20.6 36.7 %collective-permute-start.7 = (bf16[64,128,128]{2,1,0:T(8,128)(2,1)S(1)}, bf16[64,128,128]{2,1,0:T(8,128)(2,1)}, u32[]{:S(2)}, u32[]{:S(2)}) collective-permute-start(bf16[64,128,128]{2,1,0:T(8,128)(2,1)S(1)} %copy-done), channel_id=1, source_target_pairs={{0,32},{1,97},{2,34},{3,99},{4,36},{5,101},{6,38},{7,103},{8,40},{... | collective-permute-start | bytes 6291464 | tf_op jit(solution)/shard_map/ppermute | solution.py:52
  23.9 35.9 %collective-permute-start.8 = (bf16[64,128,128]{2,1,0:T(8,128)(2,1)S(1)}, bf16[64,128,128]{2,1,0:T(8,128)(2,1)}, u32[]{:S(2)}, u32[]{:S(2)}) collective-permute-start(bf16[64,128,128]{2,1,0:T(8,128)(2,1)S(1)} %copy-done), channel_id=1, source_target_pairs={{0,2},{1,7},{2,4},{3,1},{4,6},{5,3},{6,0},{7,5},{8,10},{9,15},{10,... | collective-permute-start | bytes 6291464 | tf_op jit(solution)/shard_map/ppermute | solution.py:52
  25.1 2.5 %collective-permute-start.3 = (bf16[32,4096]{1,0:T(8,128)(2,1)S(1)}, bf16[32,4096]{1,0:T(8,128)(2,1)S(1)}, u32[]{:S(2)}, u32[]{:S(2)}) collective-permute-start(bf16[32,4096]{1,0:T(8,128)(2,1)S(1)} %pad_maximum_fusion.near_ref), channel_id=1, source_target_pairs={{0,1},{1,0},{2,3},{3,2},{4,5},{5,4},{6,7},{7,6},{8,9},{9,8},{10,11... | collective-permute-start | bytes 786440 | tf_op jit(solution)/shard_map/ppermute | solution.py:57
  27.6 0.7 copy-start.4
  44.6 12.7 %collective-permute-start.9 = (bf16[128,4096]{1,0:T(8,128)(2,1)S(1)}, bf16[128,4096]{1,0:T(8,128)(2,1)}, u32[]{:S(2)}, u32[]{:S(2)}) collective-permute-start(bf16[128,4096]{1,0:T(8,128)(2,1)S(1)} %bitcast.10), channel_id=1, source_target_pairs={{0,1},{1,0},{2,3},{3,2},{4,5},{5,4},{6,7},{7,6},{8,9},{9,8},{10,11... | collective-permute-start | bytes 3145736 | tf_op jit(solution)/shard_map/ppermute | solution.py:57
  46.1 1.6 %collective-permute-start.4 = (bf16[32,4096]{1,0:T(8,128)(2,1)S(1)}, bf16[32,4096]{1,0:T(8,128)(2,1)S(1)}, u32[]{:S(2)}, u32[]{:S(2)}) collective-permute-start(bf16[32,4096]{1,0:T(8,128)(2,1)S(1)} %get-tuple-element.32), channel_id=1, source_target_pairs={{0,1},{1,0},{2,3},{3,2},{4,5},{5,4},{6,7},{7,6},{8,9},{9,8},{10,11... | collective-permute-start | bytes 786440 | tf_op jit(solution)/shard_map/ppermute | solution.py:57
  48.5 8.8 %collective-permute-start.5 = (bf16[16,4096]{1,0:T(8,128)(2,1)}, bf16[16,4096]{1,0:T(8,128)(2,1)S(1)}, u32[]{:S(2)}, u32[]{:S(2)}) collective-permute-start(bf16[16,4096]{1,0:T(8,128)(2,1)} %slice.18), channel_id=1, source_target_pairs={{0,2},{2,0},{1,3},{3,1},{4,6},{6,4},{5,7},{7,5},{8,10},{10,8},{9,1... | collective-permute-start | bytes 393224 | tf_op jit(solution)/shard_map/ppermute | solution.py:57
  64.8 2.7 %collective-permute-start.10 = (bf16[128,4096]{1,0:T(8,128)(2,1)S(1)}, bf16[128,4096]{1,0:T(8,128)(2,1)S(1)}, u32[]{:S(2)}, u32[]{:S(2)}) collective-permute-start(bf16[128,4096]{1,0:T(8,128)(2,1)S(1)} %get-tuple-element.31), channel_id=1, source_target_pairs={{0,1},{1,0},{2,3},{3,2},{4,5},{5,4},{6,7},{7,6},{8,9},{9,8},{10,11... | collective-permute-start | bytes 3145736 | tf_op jit(solution)/shard_map/ppermute | solution.py:57
  67.6 8.4 %copy-start.5 = (bf16[4096]{0:T(1024)(128)(2,1)S(1)}, bf16[4096]{0:T(1024)(128)(2,1)}, u32[]{:S(2)}) copy-start(bf16[4096]{0:T(1024)(128)(2,1)} %param.21) | copy-start | bytes 24580
  67.6 29.5 %copy-start.1 = (bf16[2,2,2,4096]{3,2,1,0:T(2,128)(2,1)S(1)}, bf16[2,2,2,4096]{3,2,1,0:T(2,128)(2,1)}, u32[]{:S(2)}) copy-start(bf16[2,2,2,4096]{3,2,1,0:T(2,128)(2,1)} %tokens_ref.1) | copy-start | bytes 196612
  67.6 29.5 %copy-start.2 = (f32[4096]{0:T(1024)S(1)}, f32[4096]{0:T(1024)}, u32[]{:S(2)}) copy-start(f32[4096]{0:T(1024)} %param.20) | copy-start | bytes 49156
  68.8 28.2 %all-to-all-start.1 = ((bf16[16,8,4096]{2,1,0:T(8,128)(2,1)}), bf16[16,8,4096]{2,1,0:T(8,128)(2,1)S(1)}, u32[]{:S(2)}, u32[]{:S(2)}) async-start(bf16[16,8,4096]{2,1,0:T(8,128)(2,1)} %bitcast.8), calls=%async_computation.1 | async-start | bytes 2097152 | tf_op jit(solution)/shard_map/all_to_all | solution.py:448

commit v4 on v3

--- a/solution.py
+++ b/solution.py
@@ -11,6 +11,7 @@
 LANES = 128
 VERY_LOW = -1e30
 CUT = 2
+SUM_BLOCKS = 4
 MIB = 2**20
 SMEM = pl.BlockSpec(memory_space=pltpu.SMEM)
 VMEM = pl.BlockSpec(memory_space=pltpu.VMEM)
@@ -368,6 +369,30 @@
     )(a, b)
 
 
+def sum_body(a_ref, b_ref, out_hbm, total, sem):
+    step = total.shape[0] // SUM_BLOCKS
+    copies = []
+    for i in range(SUM_BLOCKS):
+        at = pl.ds(i * step, step)
+        total[at] = (a_ref[at].astype(jnp.float32) + b_ref[at].astype(jnp.float32)).astype(jnp.bfloat16)
+        copies.append(pltpu.make_async_copy(total.at[at], out_hbm.at[at], sem.at[i]))
+        copies[i].start()
+    for copy in copies:
+        copy.wait()
+
+
+def sum_call(a, b):
+    return pl.pallas_call(
+        sum_body,
+        out_shape=jax.ShapeDtypeStruct(b.shape, jnp.bfloat16),
+        in_specs=[VMEM] * 2,
+        out_specs=HBM,
+        scratch_shapes=[pltpu.VMEM(b.shape, jnp.bfloat16), pltpu.SemaphoreType.DMA((SUM_BLOCKS,))],
+        compiler_params=pltpu.CompilerParams(vmem_limit_bytes=8 * MIB),
+        name="sum",
+    )(a, b)
+
+
 def end_body(tokens_ref, returned_ref, gain_ref, score_ref, next_ref, out_ref, rows):
     requests, samples, fresh, width = tokens_ref.shape
     for r in range(requests):
@@ -480,7 +505,7 @@
     place = lax.axis_index("y") * SIDE + lax.axis_index("x") // 2 * 2 + lax.axis_index("u")
     place = place.astype(jnp.int32).reshape(1)
     mine, others = mlp_call(place, visitors, other_visitors, projected[:half], projected_far, packed)
-    summed = add_call(mine, swap(others, "c"))
+    summed = sum_call(mine, swap(others, "c"))
     returned = exchange(summed.reshape(sharing, own_rows, width))
     next_hidden, sample_scores = end_call(tokens, returned, final_gain, score_weight)
     return (next_hidden, sample_scores)

time: 98.6 us -> 98.4 us (level)
    pallas_call x2 -> x1, Pallas kernels: 1.31 us -> 0.06 us  [add_call(): pl.pallas_call(add_body, out_shape=jax.ShapeDtypeStruct(b.shape, jnp.bflo...]
    pallas_call x0 -> x1, Pallas kernels: none -> 1.11 us  [sum_call(): pl.pallas_call(sum_body, out_shape=jax.ShapeDtypeStruct(b.shape, jnp.bflo...]
where the time goes in v4:
time: 98.4 us; the launch traced here: 98 us
  waiting for transfers between devices  36.6 us (37%)
  starting transfers between devices  28.8 us (29%)
  Pallas kernels  27.2 us (28%)
  local copies, waits for them, and re-layouts  2.6 us (3%)
  other arithmetic  1.88 us (2%)
    all_to_all x2, waiting for transfers between devices, exchange(): lax.all_to_all(values, AXES, 0, 0, axis_index_groups=groups, tiled=True)  21.1 us
    all_to_all x2, starting transfers between devices, exchange(): lax.all_to_all(values, AXES, 0, 0, axis_index_groups=groups, tiled=True)  16.7 us
    pallas_call x1, Pallas kernels, mixer_call(): pl.pallas_call(mixer_body, out_shape=jax.ShapeDtypeStruct((count, width),...  16.3 us
    ppermute x8, waiting for transfers between devices, swap(): return lax.ppermute(values, axes, [(i, last - i) for i in range(last + 1)])  13 us
    ppermute x8, starting transfers between devices, swap(): return lax.ppermute(values, axes, [(i, last - i) for i in range(last + 1)])  7.27 us
    pallas_call x1, Pallas kernels, mlp_call(): pl.pallas_call(mlp_body, out_shape=[jax.ShapeDtypeStruct((count, width),...  5 us
    ppermute x3, starting transfers between devices, from_neighbour(): return lax.ppermute(values, AXES, moves)  4.92 us
    pallas_call x1, Pallas kernels, start_call(): pl.pallas_call(start_body, out_shape=[jax.ShapeDtypeStruct((own_rows, wid...  3.65 us
  transfers between devices with their start and end apart: 13, of which 6 were waited for; matrix products, arithmetic and copies ran while one was open for 4% of the time, Pallas kernels for 17%

profile of v4, /device:TPU:0, one launch (start us, length us, event | category | flops | bytes accessed | tf_op | source)
XLA Modules:
  0.0 98.0 jit_solution(5751741077865543121)
XLA Ops:
  0.6 0.0 copy-start.6
  0.6 0.0 copy-start.7
  0.7 3.7 %start.1 = (bf16[8,4096]{1,0:T(8,128)(2,1)}, bf16[16,8,4096]{2,1,0:T(8,128)(2,1)}, bf16[64,128,128]{2,1,0:T(8,128)(2,1)}) custom-call(bf16[2,2,2,4096]{3,2,1,0:T(2,128)(2,1)} %tokens_ref.1, f32[1,4096]{1,0:T(1,128)} %bitcast.17, bf16[32,128,128]{2,1,0:T(8,128)(2,1)} %bitcast.16, bf16[128,4096]{1,0:T(8,128)(2,1)} %down_hbm.1), custom_call_target="tpu_custom_call" | custom-call | tf_op jit(solution)/shard_map/start/pallas_call | solution.py:111
  4.3 0.0 copy-start
  4.3 4.0 %collective-permute-start = (bf16[8,4096]{1,0:T(8,128)(2,1)}, bf16[8,4096]{1,0:T(8,128)(2,1)S(1)}, u32[]{:S(2)}, u32[]{:S(2)}) collective-permute-start(bf16[8,4096]{1,0:T(8,128)(2,1)} %get-tuple-element.17), channel_id=1, source_target_pairs={{0,4},{4,0},{1,5},{5,1},{2,6},{6,2},{3,7},{7,3},{8,12},{12,8},{9,1... | collective-permute-start | bytes 196616 | tf_op jit(solution)/shard_map/ppermute | solution.py:58
  8.4 1.0 %collective-permute-start.1 = (bf16[8,4096]{1,0:T(8,128)(2,1)}, bf16[8,4096]{1,0:T(8,128)(2,1)S(1)}, u32[]{:S(2)}, u32[]{:S(2)}) collective-permute-start(bf16[8,4096]{1,0:T(8,128)(2,1)} %get-tuple-element.17), channel_id=1, source_target_pairs={{0,2},{2,0},{1,3},{3,1},{4,6},{6,4},{5,7},{7,5},{8,10},{10,8},{9,1... | collective-permute-start | bytes 196616 | tf_op jit(solution)/shard_map/ppermute | solution.py:58
  9.4 0.0 collective-permute-start.2
  9.4 9.5 %all-to-all-start = ((bf16[16,8,4096]{2,1,0:T(8,128)(2,1)}), bf16[16,8,4096]{2,1,0:T(8,128)(2,1)S(1)}, u32[]{:S(2)}, u32[]{:S(2)}) async-start(bf16[16,8,4096]{2,1,0:T(8,128)(2,1)} %get-tuple-element.21), calls=%async_computation | async-start | bytes 2097152 | tf_op jit(solution)/shard_map/all_to_all | solution.py:473
  18.9 0.0 copy-done.6
  18.9 0.0 copy-done.7
  19.0 0.1 broadcast_add_fusion
  19.0 0.0 collective-permute-done
  19.0 0.0 collective-permute-done.1
  19.0 0.0 collective-permute-done.2
  19.0 0.9 pad_maximum_fusion.near_ref
  19.9 0.0 copy-start.3
  19.9 0.0 copy-done
  20.0 0.7 collective-permute-start.6
  20.6 3.2 %collective-permute-start.7 = (bf16[64,128,128]{2,1,0:T(8,128)(2,1)S(1)}, bf16[64,128,128]{2,1,0:T(8,128)(2,1)}, u32[]{:S(2)}, u32[]{:S(2)}) collective-permute-start(bf16[64,128,128]{2,1,0:T(8,128)(2,1)S(1)} %copy-done), channel_id=1, source_target_pairs={{0,32},{1,97},{2,34},{3,99},{4,36},{5,101},{6,38},{7,103},{8,40},{... | collective-permute-start | bytes 6291464 | tf_op jit(solution)/shard_map/ppermute | solution.py:53
  23.9 1.0 %collective-permute-start.8 = (bf16[64,128,128]{2,1,0:T(8,128)(2,1)S(1)}, bf16[64,128,128]{2,1,0:T(8,128)(2,1)}, u32[]{:S(2)}, u32[]{:S(2)}) collective-permute-start(bf16[64,128,128]{2,1,0:T(8,128)(2,1)S(1)} %copy-done), channel_id=1, source_target_pairs={{0,2},{1,7},{2,4},{3,1},{4,6},{5,3},{6,0},{7,5},{8,10},{9,15},{10,... | collective-permute-start | bytes 6291464 | tf_op jit(solution)/shard_map/ppermute | solution.py:53
  24.9 0.1 add_convert_fusion
  24.9 0.1 convert_element_type.18
  25.1 1.3 %collective-permute-start.3 = (bf16[32,4096]{1,0:T(8,128)(2,1)S(1)}, bf16[32,4096]{1,0:T(8,128)(2,1)S(1)}, u32[]{:S(2)}, u32[]{:S(2)}) collective-permute-start(bf16[32,4096]{1,0:T(8,128)(2,1)S(1)} %pad_maximum_fusion.near_ref), channel_id=1, source_target_pairs={{0,1},{1,0},{2,3},{3,2},{4,5},{5,4},{6,7},{7,6},{8,9},{9,8},{10,11... | collective-permute-start | bytes 786440 | tf_op jit(solution)/shard_map/ppermute | solution.py:58
  26.4 0.2 fusion
  26.6 0.6 pad_maximum_fusion.1.turn_ref
  27.2 0.3 collective-permute-done.3.far_ref
  27.6 0.0 copy-start.4
  27.6 0.0 copy-done.3
  27.6 0.7 copy-done.4
  28.3 16.3 %mixer.1 = bf16[64,4096]{1,0:T(8,128)(2,1)} custom-call(s32[2]{0:T(128)} %plen_ref.1, s32[2,16]{1,0:T(2,128)} %tlen_ref.1, s32[1]{0:T(128)} %bitcast.1.hid_ref, bf16[32,4096]{1,0:T(8,128)(2,1)} %copy-done.3, bf16[32,4096]{1,0:T(8,128)(2,1)} %copy-done.4, f32[2,64,128]{2,1,0:T(8,128)} %pad_maximum_fusion.1.turn_ref, bf16[3,4096,512]{2,1,0:T(8,128)(2,1)} %bitcast.13, ...), custom_call_target="tpu_custom_call" | custom-call | flops 1476395008 | bytes 29360128 | tf_op jit(solution)/shard_map/mixer/pallas_call | solution.py:254
  44.6 0.0 all-to-all-done
  44.6 0.5 collective-permute-start.9
  45.1 1.1 %fusion.7 = (bf16[32,4096]{1,0:T(8,128)(2,1)S(1)}, bf16[32,4096]{1,0:T(8,128)(2,1)S(1)}) fusion(bf16[64,4096]{1,0:T(8,128)(2,1)} %mixer.1), kind=kLoop, calls=%fused_computation.20 | loop fusion | bytes 1048576 | tf_op jit(solution)/shard_map/slice | solution.py:498
  46.1 0.2 collective-permute-start.4
  46.3 1.4 %collective-permute-done.4.b_ref = bf16[32,4096]{1,0:T(8,128)(2,1)S(1)} collective-permute-done((bf16[32,4096]{1,0:T(8,128)(2,1)S(1)}, bf16[32,4096]{1,0:T(8,128)(2,1)S(1)}, u32[]{:S(2)}, u32[]{:S(2)}) %collective-permute-start.4) | collective-permute-done | bytes 262176 | tf_op jit(solution)/shard_map/ppermute | solution.py:58
  47.7 0.1 add.75
  47.8 0.7 slice.18
  48.5 0.1 collective-permute-start.5
  48.6 8.7 %collective-permute-done.5.far_hbm = bf16[16,4096]{1,0:T(8,128)(2,1)S(1)} collective-permute-done((bf16[16,4096]{1,0:T(8,128)(2,1)}, bf16[16,4096]{1,0:T(8,128)(2,1)S(1)}, u32[]{:S(2)}, u32[]{:S(2)}) %collective-permute-start.5) | collective-permute-done | bytes 131104 | tf_op jit(solution)/shard_map/ppermute | solution.py:58
  57.3 0.0 collective-permute-done.9.other_hbm
  57.3 0.0 collective-permute-done.6.refs_1_
  57.3 0.0 collective-permute-done.7.refs_2_
  57.3 2.5 %collective-permute-done.8.refs_3_ = bf16[64,128,128]{2,1,0:T(8,128)(2,1)} collective-permute-done((bf16[64,128,128]{2,1,0:T(8,128)(2,1)S(1)}, bf16[64,128,128]{2,1,0:T(8,128)(2,1)}, u32[]{:S(2)}, u32[]{:S(2)}) %collective-permute-start.8) | collective-permute-done | bytes 2097184 | tf_op jit(solution)/shard_map/ppermute | solution.py:53
  59.8 5.0 %mlp.1 = (bf16[128,4096]{1,0:T(8,128)(2,1)S(1)}, bf16[128,4096]{1,0:T(8,128)(2,1)S(1)}) custom-call(s32[1]{0:T(128)} %bitcast.place_ref, bf16[128,4096]{1,0:T(8,128)(2,1)S(1)} %bitcast.11, bf16[128,4096]{1,0:T(8,128)(2,1)} %collective-permute-done.9.other_hbm, bf16[16,4096]{1,0:T(8,128)(2,1)S(1)} %slice.15.near_hbm, ...), custom_call_target="tpu_custom_call" | custom-call | flops 2147483648 | bytes 12582912 | tf_op jit(solution)/shard_map/mlp/pallas_call | solution.py:332
  64.8 0.1 collective-permute-start.10
  64.9 2.6 %collective-permute-done.10.b_ref = bf16[128,4096]{1,0:T(8,128)(2,1)S(1)} collective-permute-done((bf16[128,4096]{1,0:T(8,128)(2,1)S(1)}, bf16[128,4096]{1,0:T(8,128)(2,1)S(1)}, u32[]{:S(2)}, u32[]{:S(2)}) %collective-permute-start.10) | collective-permute-done | bytes 1048608 | tf_op jit(solution)/shard_map/ppermute | solution.py:58
  67.6 0.0 copy-start.5
  67.6 0.0 copy-start.1
  67.6 0.0 copy-start.2
  67.6 1.1 %sum.1 = bf16[128,4096]{1,0:T(8,128)(2,1)} custom-call(bf16[128,4096]{1,0:T(8,128)(2,1)S(1)} %get-tuple-element.30.a_ref, bf16[128,4096]{1,0:T(8,128)(2,1)S(1)} %collective-permute-done.10.b_ref), custom_call_target="tpu_custom_call" | custom-call | tf_op jit(solution)/shard_map/sum/pallas_call | solution.py:385
  68.7 7.1 %all-to-all-start.1 = ((bf16[16,8,4096]{2,1,0:T(8,128)(2,1)}), bf16[16,8,4096]{2,1,0:T(8,128)(2,1)S(1)}, u32[]{:S(2)}, u32[]{:S(2)}) async-start(bf16[16,8,4096]{2,1,0:T(8,128)(2,1)} %bitcast.8), calls=%async_computation.1 | async-start | bytes 2097152 | tf_op jit(solution)/shard_map/all_to_all | solution.py:473
  75.8 0.0 copy-done.5
  75.8 21.1 %all-to-all-done.1.returned_ref = bf16[16,8,4096]{2,1,0:T(8,128)(2,1)S(1)} async-done(((bf16[16,8,4096]{2,1,0:T(8,128)(2,1)}), bf16[16,8,4096]{2,1,0:T(8,128)(2,1)S(1)}, u32[]{:S(2)}, u32[]{:S(2)}) %all-to-all-start.1) | async-done | bytes 1048608 | tf_op jit(solution)/shard_map/all_to_all | solution.py:473
  96.9 0.0 copy-done.1
  96.9 0.0 copy-done.2
  96.9 1.1 %end.1 = (bf16[2,2,2,4096]{3,2,1,0:T(2,128)(2,1)}, f32[2,2,2]{2,1,0:T(2,128)}) custom-call(bf16[2,2,2,4096]{3,2,1,0:T(2,128)(2,1)S(1)} %copy-done.1, bf16[16,8,4096]{2,1,0:T(8,128)(2,1)S(1)} %all-to-all-done.1.returned_ref, f32[1,4096]{1,0:T(1,128)S(1)} %bitcast.12, bf16[1,4096]{1,0:T(2,128)(2,1)S(1)} %reshape.250.score_ref), custom_call_target="tpu_custom_call" | custom-call | tf_op jit(solution)/shard_map/end/pallas_call | solution.py:420
  (4 shorter events, 0.0 us)
Async XLA Ops:
  0.6 18.3 %copy-start.6 = (s32[2,16]{1,0:T(2,128)S(1)}, s32[2,16]{1,0:T(2,128)}, u32[]{:S(2)}) copy-start(s32[2,16]{1,0:T(2,128)} %tlen_ref.1) | copy-start | bytes 388
  0.6 18.3 %copy-start.7 = (s32[2]{0:T(128)S(1)}, s32[2]{0:T(128)}, u32[]{:S(2)}) copy-start(s32[2]{0:T(128)} %plen_ref.1) | copy-start | bytes 28
  4.3 15.6 %copy-start = (bf16[64,128,128]{2,1,0:T(8,128)(2,1)S(1)}, bf16[64,128,128]{2,1,0:T(8,128)(2,1)}, u32[]{:S(2)}) copy-start(bf16[64,128,128]{2,1,0:T(8,128)(2,1)} %get-tuple-element.26.refs_0_) | copy-start | bytes 6291460
  4.3 14.7 %collective-permute-start = (bf16[8,4096]{1,0:T(8,128)(2,1)}, bf16[8,4096]{1,0:T(8,128)(2,1)S(1)}, u32[]{:S(2)}, u32[]{:S(2)}) collective-permute-start(bf16[8,4096]{1,0:T(8,128)(2,1)} %get-tuple-element.17), channel_id=1, source_target_pairs={{0,4},{4,0},{1,5},{5,1},{2,6},{6,2},{3,7},{7,3},{8,12},{12,8},{9,1... | collective-permute-start | bytes 196616 | tf_op jit(solution)/shard_map/ppermute | solution.py:58
  8.4 10.7 %collective-permute-start.1 = (bf16[8,4096]{1,0:T(8,128)(2,1)}, bf16[8,4096]{1,0:T(8,128)(2,1)S(1)}, u32[]{:S(2)}, u32[]{:S(2)}) collective-permute-start(bf16[8,4096]{1,0:T(8,128)(2,1)} %get-tuple-element.17), channel_id=1, source_target_pairs={{0,2},{2,0},{1,3},{3,1},{4,6},{6,4},{5,7},{7,5},{8,10},{10,8},{9,1... | collective-permute-start | bytes 196616 | tf_op jit(solution)/shard_map/ppermute | solution.py:58
  9.4 9.7 %collective-permute-start.2 = (bf16[8,4096]{1,0:T(8,128)(2,1)}, bf16[8,4096]{1,0:T(8,128)(2,1)}, u32[]{:S(2)}, u32[]{:S(2)}) collective-permute-start(bf16[8,4096]{1,0:T(8,128)(2,1)} %get-tuple-element.17), channel_id=1, source_target_pairs={{0,6},{2,4},{4,2},{6,0},{1,7},{3,5},{5,3},{7,1},{8,14},{10,12},{12... | collective-permute-start | bytes 196616 | tf_op jit(solution)/shard_map/ppermute | solution.py:58
  9.4 35.2 %all-to-all-start = ((bf16[16,8,4096]{2,1,0:T(8,128)(2,1)}), bf16[16,8,4096]{2,1,0:T(8,128)(2,1)S(1)}, u32[]{:S(2)}, u32[]{:S(2)}) async-start(bf16[16,8,4096]{2,1,0:T(8,128)(2,1)} %get-tuple-element.21), calls=%async_computation | async-start | bytes 2097152 | tf_op jit(solution)/shard_map/all_to_all | solution.py:473
  19.9 7.6 %copy-start.3 = (bf16[32,4096]{1,0:T(8,128)(2,1)}, bf16[32,4096]{1,0:T(8,128)(2,1)S(1)}, u32[]{:S(2)}) copy-start(bf16[32,4096]{1,0:T(8,128)(2,1)S(1)} %pad_maximum_fusion.near_ref) | copy-start | bytes 786436
  20.0 37.3 %collective-permute-start.6 = (bf16[64,128,128]{2,1,0:T(8,128)(2,1)S(1)}, bf16[64,128,128]{2,1,0:T(8,128)(2,1)}, u32[]{:S(2)}, u32[]{:S(2)}) collective-permute-start(bf16[64,128,128]{2,1,0:T(8,128)(2,1)S(1)} %copy-done), channel_id=1, source_target_pairs={{0,8},{1,25},{2,10},{3,27},{4,12},{5,29},{6,14},{7,31},{8,16},{9,1... | collective-permute-start | bytes 6291464 | tf_op jit(solution)/shard_map/ppermute | solution.py:53
  20.6 36.7 %collective-permute-start.7 = (bf16[64,128,128]{2,1,0:T(8,128)(2,1)S(1)}, bf16[64,128,128]{2,1,0:T(8,128)(2,1)}, u32[]{:S(2)}, u32[]{:S(2)}) collective-permute-start(bf16[64,128,128]{2,1,0:T(8,128)(2,1)S(1)} %copy-done), channel_id=1, source_target_pairs={{0,32},{1,97},{2,34},{3,99},{4,36},{5,101},{6,38},{7,103},{8,40},{... | collective-permute-start | bytes 6291464 | tf_op jit(solution)/shard_map/ppermute | solution.py:53
  23.9 35.9 %collective-permute-start.8 = (bf16[64,128,128]{2,1,0:T(8,128)(2,1)S(1)}, bf16[64,128,128]{2,1,0:T(8,128)(2,1)}, u32[]{:S(2)}, u32[]{:S(2)}) collective-permute-start(bf16[64,128,128]{2,1,0:T(8,128)(2,1)S(1)} %copy-done), channel_id=1, source_target_pairs={{0,2},{1,7},{2,4},{3,1},{4,6},{5,3},{6,0},{7,5},{8,10},{9,15},{10,... | collective-permute-start | bytes 6291464 | tf_op jit(solution)/shard_map/ppermute | solution.py:53
  25.1 2.5 %collective-permute-start.3 = (bf16[32,4096]{1,0:T(8,128)(2,1)S(1)}, bf16[32,4096]{1,0:T(8,128)(2,1)S(1)}, u32[]{:S(2)}, u32[]{:S(2)}) collective-permute-start(bf16[32,4096]{1,0:T(8,128)(2,1)S(1)} %pad_maximum_fusion.near_ref), channel_id=1, source_target_pairs={{0,1},{1,0},{2,3},{3,2},{4,5},{5,4},{6,7},{7,6},{8,9},{9,8},{10,11... | collective-permute-start | bytes 786440 | tf_op jit(solution)/shard_map/ppermute | solution.py:58
  27.6 0.7 copy-start.4
  44.6 12.7 %collective-permute-start.9 = (bf16[128,4096]{1,0:T(8,128)(2,1)S(1)}, bf16[128,4096]{1,0:T(8,128)(2,1)}, u32[]{:S(2)}, u32[]{:S(2)}) collective-permute-start(bf16[128,4096]{1,0:T(8,128)(2,1)S(1)} %bitcast.10), channel_id=1, source_target_pairs={{0,1},{1,0},{2,3},{3,2},{4,5},{5,4},{6,7},{7,6},{8,9},{9,8},{10,11... | collective-permute-start | bytes 3145736 | tf_op jit(solution)/shard_map/ppermute | solution.py:58
  46.1 1.6 %collective-permute-start.4 = (bf16[32,4096]{1,0:T(8,128)(2,1)S(1)}, bf16[32,4096]{1,0:T(8,128)(2,1)S(1)}, u32[]{:S(2)}, u32[]{:S(2)}) collective-permute-start(bf16[32,4096]{1,0:T(8,128)(2,1)S(1)} %get-tuple-element.32), channel_id=1, source_target_pairs={{0,1},{1,0},{2,3},{3,2},{4,5},{5,4},{6,7},{7,6},{8,9},{9,8},{10,11... | collective-permute-start | bytes 786440 | tf_op jit(solution)/shard_map/ppermute | solution.py:58
  48.5 8.8 %collective-permute-start.5 = (bf16[16,4096]{1,0:T(8,128)(2,1)}, bf16[16,4096]{1,0:T(8,128)(2,1)S(1)}, u32[]{:S(2)}, u32[]{:S(2)}) collective-permute-start(bf16[16,4096]{1,0:T(8,128)(2,1)} %slice.18), channel_id=1, source_target_pairs={{0,2},{2,0},{1,3},{3,1},{4,6},{6,4},{5,7},{7,5},{8,10},{10,8},{9,1... | collective-permute-start | bytes 393224 | tf_op jit(solution)/shard_map/ppermute | solution.py:58
  64.8 2.7 %collective-permute-start.10 = (bf16[128,4096]{1,0:T(8,128)(2,1)S(1)}, bf16[128,4096]{1,0:T(8,128)(2,1)S(1)}, u32[]{:S(2)}, u32[]{:S(2)}) collective-permute-start(bf16[128,4096]{1,0:T(8,128)(2,1)S(1)} %get-tuple-element.31), channel_id=1, source_target_pairs={{0,1},{1,0},{2,3},{3,2},{4,5},{5,4},{6,7},{7,6},{8,9},{9,8},{10,11... | collective-permute-start | bytes 3145736 | tf_op jit(solution)/shard_map/ppermute | solution.py:58
  67.6 8.2 %copy-start.5 = (bf16[4096]{0:T(1024)(128)(2,1)S(1)}, bf16[4096]{0:T(1024)(128)(2,1)}, u32[]{:S(2)}) copy-start(bf16[4096]{0:T(1024)(128)(2,1)} %param.21) | copy-start | bytes 24580
  67.6 29.3 %copy-start.1 = (bf16[2,2,2,4096]{3,2,1,0:T(2,128)(2,1)S(1)}, bf16[2,2,2,4096]{3,2,1,0:T(2,128)(2,1)}, u32[]{:S(2)}) copy-start(bf16[2,2,2,4096]{3,2,1,0:T(2,128)(2,1)} %tokens_ref.1) | copy-start | bytes 196612
  67.6 29.3 %copy-start.2 = (f32[4096]{0:T(1024)S(1)}, f32[4096]{0:T(1024)}, u32[]{:S(2)}) copy-start(f32[4096]{0:T(1024)} %param.20) | copy-start | bytes 49156
  68.7 28.2 %all-to-all-start.1 = ((bf16[16,8,4096]{2,1,0:T(8,128)(2,1)}), bf16[16,8,4096]{2,1,0:T(8,128)(2,1)S(1)}, u32[]{:S(2)}, u32[]{:S(2)}) async-start(bf16[16,8,4096]{2,1,0:T(8,128)(2,1)} %bitcast.8), calls=%async_computation.1 | async-start | bytes 2097152 | tf_op jit(solution)/shard_map/all_to_all | solution.py:473
